TPU v7x, 32 devices: a whole 2x2x4 slice. The times are simulated.
32 devices in a mesh: row: 4 (over z), col: 8 (over y, x, core).
Axes of the slice: x: 2, y: 2, z: 4, core: 2. Of those that a mesh axis runs over, the one named last changes fastest.
Arguments:
- pair_state: bfloat16 [384, 384, 128], P('row', 'col'), may hold values from -40 to 40
- seq_state: bfloat16 [384, 1024], P('row', 'col'), may hold values from -40 to 40
- residue_index: int32 [384], replicated, may hold values from 0 to 1535, as said below
- residue_mask: int32 [384], replicated, may hold values from 0 to 1, as said below
- position_table: bfloat16 [66, 128], replicated, may hold values from -4 to 4
- attention_gain: float32 [2, 1024], replicated, may hold values from 0.1 to 1.9
- bias_norm_gain: float32 [2, 128], replicated, may hold values from 0.1 to 1.9
- query_weight: bfloat16 [2, 1024, 1024], P(None, None, 'col'), may hold values from -16 to 16
- key_weight: bfloat16 [2, 1024, 1024], P(None, None, 'col'), may hold values from -1 to 1
- value_weight: bfloat16 [2, 1024, 1024], P(None, None, 'col'), may hold values from -0.1875 to 0.1875
- gate_weight: bfloat16 [2, 1024, 1024], P(None, None, 'col'), may hold values from -0.1875 to 0.1875
- out_weight: bfloat16 [2, 1024, 1024], P(None, None, 'col'), may hold values from -0.75 to 0.75
- bias_weight: bfloat16 [2, 128, 32], replicated, may hold values from -1.5 to 1.5
- outer_gain: float32 [2, 1024], replicated, may hold values from 0.1 to 1.9
- outer_weight: bfloat16 [2, 1024, 128], replicated, may hold values from -0.1875 to 0.1875
- outer_out_weight: bfloat16 [2, 128, 128], replicated, may hold values from -0.5 to 0.5
- transition_gain: float32 [2, 128], replicated, may hold values from 0.1 to 1.9
- up_weight: bfloat16 [2, 128, 512], replicated, may hold values from -0.5 to 0.5
- down_weight: bfloat16 [2, 512, 128], replicated, may hold values from -0.25 to 0.25
- distance_weight: bfloat16 [128, 64], replicated, may hold values from -0.5 to 0.5
Outputs:
- distogram: bfloat16 [384, 384, 64], P('row', 'col')
- seq_out: bfloat16 [384, 1024], P('row', 'col')
Inputs may be any that keep to these rules, and one draw needn't show every extreme that they name: `residue_index`: strictly increasing; the first entry is 0 and the last is 1535. `residue_mask`: 1 on a prefix of 192 to 383 residues and 0 after it.
All inputs are finite; a program needn't handle non-finite values.
Results may differ from a plain program's by a relative error of at most 0.028.
Values may be sent and summed in bfloat16 or wider, within the bound.
A program may use at most 64 MiB of HBM per device.

v0:
```python
import jax
import jax.numpy as jnp
from jax import lax
from jax.experimental import pallas as pl
from jax.experimental.pallas import tpu as pltpu
from jax.sharding import PartitionSpec as P

HEAD_DIM = 32
RELPOS_MAX = 32
MESH = pl.DeviceIdType.MESH


def normalize(values, weight_gain):
    average = jnp.mean(values, axis=-1, keepdims=True)
    centred = values - average
    spread = jnp.mean(centred * centred, axis=-1, keepdims=True)
    return centred * lax.rsqrt(spread + 1e-05) * weight_gain


def full_spec():
    return pl.BlockSpec(memory_space=pltpu.VMEM)


def lane_join(stacked_ref):
    return jnp.concatenate([stacked_ref[k] for k in range(stacked_ref.shape[0])], axis=1)


def spread(source, target, axis, send_sem, recv_sem):
    total, me = lax.axis_size(axis), lax.axis_index(axis)
    copies = []
    for step in range(1, total):
        peer = lax.rem(me + step, total)
        copies.append(
            pltpu.make_async_remote_copy(
                src_ref=source(peer),
                dst_ref=target(me),
                send_sem=send_sem.at[step - 1],
                recv_sem=recv_sem.at[step - 1],
                device_id={axis: peer},
                device_id_type=MESH,
            )
        )
    for copy in copies:
        copy.start()
    return copies


def finish(copies):
    for copy in copies:
        copy.wait()


def sequence_step(
    layer, seq_tile, seq_all, bias_send, live_column, gains, weights, outer_weight, own_id
):
    nr, nc = lax.axis_size("row"), lax.axis_size("col")
    tr, width = seq_tile.shape
    heads, tc, lanes = bias_send.shape
    hl = heads // nc
    length = nr * tr
    cs = outer_weight.shape[1]
    wide = outer_weight.shape[2]
    first = seq_all is None
    score_scale = HEAD_DIM ** (-0.5)

    def kernel(*refs):
        it = iter(refs)
        seq_ref = next(it)
        seq_all_ref = None if first else next(it)
        bias_ref, live_ref, gain_ref, outer_gain_ref = (next(it) for _ in range(4))
        weight_hbm = [next(it) for _ in range(6)]
        seq_out, seq_out_all, left_out, right_out = (next(it) for _ in range(4))
        weight_refs = [next(it) for _ in range(6)]
        gathered, kv_all, bias_all, gated_all, right_send = (next(it) for _ in range(5))
        weight_sem = next(it)
        col_send, col_recv, row_send, row_recv = (next(it) for _ in range(4))

        loads = [
            pltpu.make_async_copy(weight_hbm[k].at[layer], weight_refs[k], weight_sem.at[k])
            for k in range(6)
        ]
        for load in loads:
            load.start()
        row, col = lax.axis_index("row"), lax.axis_index("col")
        barrier = pltpu.get_barrier_semaphore()
        for axis, total, me in (("col", nc, col), ("row", nr, row)):
            for step in range(1, total):
                pl.semaphore_signal(
                    barrier,
                    inc=1,
                    device_id={axis: lax.rem(me + step, total)},
                    device_id_type=MESH,
                )
        pl.semaphore_wait(barrier, nc + nr - 2)
        if first:
            seq_copies = spread(
                lambda peer: seq_ref,
                lambda me: gathered.at[me],
                "col",
                col_send.at[0],
                col_recv.at[0],
            )
        bias_copies = spread(
            lambda peer: bias_ref.at[pl.ds(peer * hl, hl)],
            lambda me: bias_all.at[me],
            "col",
            col_send.at[1],
            col_recv.at[1],
        )
        bias_all[col] = bias_ref[pl.ds(col * hl, hl)]
        if first:
            gathered[col] = seq_ref[...]
            finish(seq_copies)
            entering = lane_join(gathered)
        else:
            entering = lane_join(seq_all_ref)
        normed = normalize(entering.astype(jnp.float32), gain_ref[pl.ds(layer, 1), :]).astype(
            jnp.bfloat16
        )

        def product(value, k):
            return jnp.dot(value, weight_refs[k][...], preferred_element_type=jnp.float32)

        loads[1].wait()
        kv_all[row, 0] = product(normed, 1).astype(jnp.bfloat16)
        loads[2].wait()
        kv_all[row, 1] = product(normed, 2).astype(jnp.bfloat16)
        kv_copies = spread(
            lambda peer: kv_all.at[row],
            lambda me: kv_all.at[me],
            "row",
            row_send.at[0],
            row_recv.at[0],
        )
        loads[0].wait()
        queries = (product(normed, 0) * score_scale).astype(jnp.bfloat16)
        loads[3].wait()
        gating = jax.nn.sigmoid(product(normed, 3))
        head_of = lax.broadcasted_iota(jnp.int32, (tr, width), 1) // HEAD_DIM
        finish(kv_copies)
        finish(bias_copies)
        keys = kv_all[:, 0].reshape(length, width)
        values = kv_all[:, 1].reshape(length, width)
        live = live_ref[...] > 0
        attended = jnp.zeros((tr, width), jnp.float32)
        for head in range(hl):
            own = head_of == head
            query = jnp.where(own, queries.astype(jnp.float32), 0.0).astype(jnp.bfloat16)
            scores = lax.dot_general(
                keys, query, (((1,), (1,)), ((), ())), preferred_element_type=jnp.float32
            )
            bias = bias_all[:, head].reshape(length, lanes)[:, :tr]
            scores = jnp.where(live, scores + bias.astype(jnp.float32), -jnp.inf)
            shifted = jnp.exp(scores - jnp.max(scores, axis=0, keepdims=True))
            share = (shifted / jnp.sum(shifted, axis=0, keepdims=True)).astype(jnp.bfloat16)
            mixed = lax.dot_general(
                share, values, (((0,), (0,)), ((), ())), preferred_element_type=jnp.float32
            )
            attended = jnp.where(own, mixed, attended)
        gated_all[col] = (gating * attended).astype(jnp.bfloat16)
        finish(
            spread(
                lambda peer: gated_all.at[col],
                lambda me: gated_all.at[me],
                "col",
                col_send.at[2],
                col_recv.at[2],
            )
        )
        loads[4].wait()
        leaving = (seq_ref[...].astype(jnp.float32) + product(lane_join(gated_all), 4)).astype(
            jnp.bfloat16
        )
        seq_out_all[col] = leaving
        seq_out[...] = leaving
        finish(
            spread(
                lambda peer: seq_out_all.at[col],
                lambda me: seq_out_all.at[me],
                "col",
                col_send.at[3],
                col_recv.at[3],
            )
        )
        outer_in = normalize(
            lane_join(seq_out_all).astype(jnp.float32), outer_gain_ref[pl.ds(layer, 1), :]
        ).astype(jnp.bfloat16)
        loads[5].wait()
        projected = product(outer_in, 5)
        left_out[...] = projected.astype(jnp.bfloat16)
        parts = tr // tc
        holder = lax.div(col, parts)
        right_send[...] = left_out[pl.ds(pl.multiple_of(lax.rem(col, parts) * tc, 16), tc), :]
        right_copies = [
            pltpu.make_async_remote_copy(
                src_ref=right_send,
                dst_ref=right_out,
                send_sem=row_send.at[1, step - 1],
                recv_sem=row_recv.at[1, 0],
                device_id={"row": lax.rem(row + step, nr)},
                device_id_type=MESH,
            )
            for step in range(1, nr)
        ]

        @pl.when(row == holder)
        def _():
            for copy in right_copies:
                copy.start()
            right_out[...] = right_send[...]
            for copy in right_copies:
                copy.wait_send()

        pl.when(row != holder)(right_copies[0].wait_recv)

    operands = [seq_tile] + ([] if first else [seq_all]) + [bias_send, live_column, *gains]
    specs = [full_spec()] * len(operands) + [pl.BlockSpec(memory_space=pl.ANY)] * 6
    bf16 = jnp.bfloat16
    return pl.pallas_call(
        kernel,
        out_shape=(
            jax.ShapeDtypeStruct((tr, width), bf16),
            jax.ShapeDtypeStruct((nc, tr, width), bf16),
            jax.ShapeDtypeStruct((tr, wide), bf16),
            jax.ShapeDtypeStruct((tc, wide), bf16),
        ),
        in_specs=specs,
        out_specs=(full_spec(),) * 4,
        scratch_shapes=[pltpu.VMEM((cs, width), bf16)] * 5
        + [
            pltpu.VMEM((cs, wide), bf16),
            pltpu.VMEM((nc, tr, width), bf16),
            pltpu.VMEM((nr, 2, tr, width), bf16),
            pltpu.VMEM((nc, hl, tc, lanes), bf16),
            pltpu.VMEM((nc, tr, width), bf16),
            pltpu.VMEM((tc, wide), bf16),
            pltpu.SemaphoreType.DMA((6,)),
            pltpu.SemaphoreType.DMA((4, nc - 1)),
            pltpu.SemaphoreType.DMA((4, nc - 1)),
            pltpu.SemaphoreType.DMA((2, nr - 1)),
            pltpu.SemaphoreType.DMA((2, nr - 1)),
        ],
        compiler_params=pltpu.CompilerParams(collective_id=own_id, has_side_effects=True),
    )(*operands, *weights, outer_weight)


def bias_rows(pair_ref, gain, weight, mixed_ref, out_ref, tr, tc):
    heads = weight.shape[0]

    @pl.loop(0, tc, unroll=12)
    def _(j):
        normed = normalize(pair_ref[pl.ds(j, tr, stride=tc), :], gain).astype(jnp.bfloat16)
        mixed_ref[pl.ds(j * heads, heads), 0:tr] = lax.dot_general(
            weight, normed, (((1,), (1,)), ((), ())), preferred_element_type=jnp.float32
        )

    for head in range(heads):
        out_ref[head] = mixed_ref[pl.ds(head, tc, stride=heads), :].astype(jnp.bfloat16)


def bias_step(layer, pair_flat, tr, tc, bias_norm_gain, bias_weight_t):
    heads = bias_weight_t.shape[1]
    lanes = (tr + 127) // 128 * 128

    def kernel(pair_ref, gain_ref, weight_ref, out_ref, mixed_ref):
        bias_rows(pair_ref, gain_ref[pl.ds(layer, 1), :], weight_ref[layer], mixed_ref, out_ref, tr, tc)

    return pl.pallas_call(
        kernel,
        out_shape=jax.ShapeDtypeStruct((heads, tc, lanes), jnp.bfloat16),
        in_specs=[full_spec()] * 3,
        out_specs=full_spec(),
        scratch_shapes=[pltpu.VMEM((tc * heads, lanes), jnp.float32)],
    )(pair_flat, bias_norm_gain, bias_weight_t)


def pair_rows(layer, pair_ref, left_ref, right_ref, mats, transition_ref, duplicated_ref, tr, tc):
    channels = pair_ref.shape[1]
    rows = 8
    outer_ref, up_ref, down_ref = mats
    low = lax.broadcasted_iota(jnp.int32, (1, channels), 1) < channels // 2
    left = left_ref[...].astype(jnp.float32)
    duplicated_ref[...] = jnp.where(low, left, pltpu.roll(left, channels // 2, axis=1))
    right = right_ref[...].astype(jnp.float32)
    right = jnp.where(low, pltpu.roll(right, channels // 2, axis=1), right)[None]
    gain = transition_ref[pl.ds(layer, 1), :]

    def update(first, last, store):
        @pl.loop(first // rows, last // rows, unroll=3)
        def _(step):
            at = pl.ds(pl.multiple_of(step * (rows * tc), rows * tc), rows * tc)
            left = duplicated_ref[pl.ds(pl.multiple_of(step * rows, rows), rows), :][:, None, :]
            features = jnp.where(low[None], left * right, left - right)
            features = features.reshape(rows * tc, channels).astype(jnp.bfloat16)
            middle = pair_ref[at, :].astype(jnp.float32) + jnp.dot(
                features, outer_ref[layer], preferred_element_type=jnp.float32
            )
            normed = normalize(middle, gain).astype(jnp.bfloat16)
            hidden = jnp.maximum(
                jnp.dot(normed, up_ref[layer], preferred_element_type=jnp.float32), 0.0
            ).astype(jnp.bfloat16)
            store(
                at,
                (
                    middle + jnp.dot(hidden, down_ref[layer], preferred_element_type=jnp.float32)
                ).astype(jnp.bfloat16),
            )

    return update


def pair_step(layer, pair_flat, left, right, tr, tc, mats, gains, bias_weight_t):
    channels = pair_flat.shape[1]
    heads = bias_weight_t.shape[1]
    lanes = (tr + 127) // 128 * 128

    def kernel(
        pair_ref,
        left_ref,
        right_ref,
        outer_ref,
        up_ref,
        down_ref,
        transition_ref,
        bias_gain_ref,
        bias_weight_ref,
        out_ref,
        bias_ref,
        fresh_ref,
        mixed_ref,
        duplicated_ref,
    ):
        def store(at, fresh):
            out_ref[at, :] = fresh
            fresh_ref[at, :] = fresh.astype(jnp.float32)

        mats_refs = (outer_ref, up_ref, down_ref)
        update = pair_rows(
            layer, pair_ref, left_ref, right_ref, mats_refs, transition_ref, duplicated_ref, tr, tc
        )
        update(0, tr, store)
        bias_rows(
            fresh_ref,
            bias_gain_ref[pl.ds(layer + 1, 1), :],
            bias_weight_ref[layer + 1],
            mixed_ref,
            bias_ref,
            tr,
            tc,
        )

    operands = (pair_flat, left, right, *mats, *gains, bias_weight_t)
    return pl.pallas_call(
        kernel,
        out_shape=(
            jax.ShapeDtypeStruct((tr * tc, channels), jnp.bfloat16),
            jax.ShapeDtypeStruct((heads, tc, lanes), jnp.bfloat16),
        ),
        in_specs=[full_spec()] * len(operands),
        out_specs=(full_spec(),) * 2,
        scratch_shapes=[
            pltpu.VMEM((tr * tc, channels), jnp.float32),
            pltpu.VMEM((tc * heads, lanes), jnp.float32),
            pltpu.VMEM((tr, channels), jnp.float32),
        ],
    )(*operands)


def last_step(layer, pair_flat, left, right, tile_rows, tile_cols, mats, gain, bins_pair, own_id):
    nr, nc = lax.axis_size("row"), lax.axis_size("col")
    parts = tile_rows // tile_cols
    half = tile_cols // 2
    channels = pair_flat.shape[1]
    width = bins_pair.shape[2]
    bin_count = width // 2
    count = half * tile_cols
    depth = count // nc

    def kernel(
        pair_ref,
        left_ref,
        right_ref,
        outer_ref,
        up_ref,
        down_ref,
        gain_ref,
        bins_ref,
        final_ref,
        flat_ref,
        logit_ref,
        fresh_ref,
        duplicated_ref,
        spread_ref,
        moved_ref,
        landed_ref,
        wide_ref,
        send_1,
        send_2,
        send_3,
        recv_1,
        recv_2,
        recv_3,
    ):
        row, col = lax.axis_index("row"), lax.axis_index("col")
        barrier = pltpu.get_barrier_semaphore()
        for axis, total, me in (("col", nc, col), ("row", nr, row)):
            for step in range(1, total):
                pl.semaphore_signal(
                    barrier,
                    inc=1,
                    device_id={axis: lax.rem(me + step, total)},
                    device_id_type=MESH,
                )
        pl.semaphore_wait(barrier, nc + nr - 2)

        def store(at, fresh):
            fresh_ref[at, :] = fresh.astype(jnp.float32)
            logit_ref[at, :] = jnp.dot(
                fresh, bins_ref[0], preferred_element_type=jnp.float32
            ).astype(jnp.bfloat16)

        update = pair_rows(
            layer,
            pair_ref,
            left_ref,
            right_ref,
            (outer_ref, up_ref, down_ref),
            gain_ref,
            duplicated_ref,
            tile_rows,
            tile_cols,
        )

        def away(source, target, send, recv, axis, peer):
            return pltpu.make_async_remote_copy(
                src_ref=source,
                dst_ref=target,
                send_sem=send,
                recv_sem=recv,
                device_id={axis: peer},
                device_id_type=MESH,
            )

        sent = []

        def forward(source, target, send, recv, axis, peer, me):
            remote = away(source, target, send, recv, axis, peer)
            stay = pltpu.make_async_copy(source, target, recv)
            same = peer == me
            pl.when(jnp.logical_not(same))(remote.start)
            pl.when(same)(stay.start)
            sent.append((same, remote))

        def arrive(target, recv):
            pltpu.make_async_copy(target, target, recv).wait()

        for part in range(parts):
            update(part * tile_cols, (part + 1) * tile_cols, store)
            near = fresh_ref[pl.ds(part * 2 * count, count), :].astype(jnp.bfloat16)
            far = fresh_ref[pl.ds((part * 2 + 1) * count, count), :].astype(jnp.bfloat16)
            packed = jnp.dot(near, bins_ref[0], preferred_element_type=jnp.float32) + jnp.dot(
                far, bins_ref[1], preferred_element_type=jnp.float32
            )
            for piece in range(nc):
                flat_ref[part, piece] = packed[piece * depth : (piece + 1) * depth].astype(
                    jnp.bfloat16
                )
            for step in range(1, nc):
                peer = lax.rem(col + step, nc)
                remote = away(
                    flat_ref.at[part, peer],
                    spread_ref.at[col, part],
                    send_1.at[step, part],
                    recv_1.at[col, part],
                    "col",
                    peer,
                )
                remote.start()
                sent.append((None, remote))
        for part in range(parts):
            for step in range(nc):
                origin = lax.rem(col + nc - step, nc)
                peer, slot = lax.div(origin, parts), lax.rem(origin, parts)
                if step:
                    arrive(spread_ref.at[origin, part], recv_1.at[origin, part])
                forward(
                    spread_ref.at[origin, part] if step else flat_ref.at[part, col],
                    moved_ref.at[row, slot, part],
                    send_2.at[step, part],
                    recv_2.at[row, slot, part],
                    "row",
                    peer,
                    row,
                )
        for step in range(nr):
            origin = lax.rem(row + step, nr)
            for slot in range(parts):
                for part in range(parts):
                    arrive(moved_ref.at[origin, slot, part], recv_2.at[origin, slot, part])
                    forward(
                        moved_ref.at[origin, slot, part],
                        landed_ref.at[col, slot],
                        send_3.at[step, slot, part],
                        recv_3.at[col, slot],
                        "col",
                        origin * parts + part,
                        col,
                    )
        for slot in range(parts):
            for piece in range(nc):
                arrive(landed_ref.at[piece, slot], recv_3.at[piece, slot])
                wide_ref[piece * depth : (piece + 1) * depth, :] = landed_ref[
                    piece, slot
                ].astype(jnp.float32)

            @pl.loop(0, tile_cols, unroll=8)
            def _(i, slot=slot):
                packed = wide_ref[pl.ds(i, half, stride=tile_cols), :]
                other = pltpu.roll(packed, width - bin_count, axis=1)
                flipped = jnp.concatenate([packed, other], axis=0)
                at = pl.multiple_of((slot * tile_cols + i) * tile_cols, 16)
                own = logit_ref[pl.ds(at, tile_cols), :].astype(jnp.float32)
                final = ((own + flipped) * 0.5).astype(jnp.bfloat16)
                final_ref[slot * tile_cols + i] = final[:, :bin_count]

        for same, remote in sent:
            if same is None:
                remote.wait_send()
            else:
                pl.when(jnp.logical_not(same))(remote.wait_send)

    operands = (pair_flat, left, right, *mats, gain, bins_pair)
    bf16 = jnp.bfloat16
    dma = pltpu.SemaphoreType.DMA
    return pl.pallas_call(
        kernel,
        out_shape=jax.ShapeDtypeStruct((tile_rows, tile_cols, bin_count), jnp.bfloat16),
        in_specs=[full_spec()] * len(operands),
        out_specs=full_spec(),
        scratch_shapes=[
            pltpu.VMEM((parts, nc, depth, width), bf16),
            pltpu.VMEM((tile_rows * tile_cols, width), bf16),
            pltpu.VMEM((tile_rows * tile_cols, channels), jnp.float32),
            pltpu.VMEM((tile_rows, channels), jnp.float32),
            pltpu.VMEM((nc, parts, depth, width), bf16),
            pltpu.VMEM((nr, parts, parts, depth, width), bf16),
            pltpu.VMEM((nc, parts, depth, width), bf16),
            pltpu.VMEM((nc * depth, width), jnp.float32),
            dma((nc, parts)),
            dma((nc, parts)),
            dma((nr, parts, parts)),
            dma((nc, parts)),
            dma((nr, parts, parts)),
            dma((nc, parts)),
        ],
        compiler_params=pltpu.CompilerParams(collective_id=own_id, has_side_effects=True),
    )(*operands)


def per_device(
    pair_state,
    seq_state,
    residue_index,
    residue_mask,
    position_table,
    attention_gain,
    bias_norm_gain,
    query_weight,
    key_weight,
    value_weight,
    gate_weight,
    out_weight,
    bias_weight,
    outer_gain,
    outer_weight,
    outer_out_weight,
    transition_gain,
    up_weight,
    down_weight,
    distance_weight,
):
    col_total = lax.axis_size("col")
    tile_rows, tile_cols, channels = pair_state.shape
    length = tile_cols * col_total
    row_first = lax.axis_index("row") * tile_rows
    col_first = lax.axis_index("col") * tile_cols
    coded = jnp.where(residue_mask > 0, residue_index, -1)
    row_pos = lax.dynamic_slice_in_dim(coded, row_first, tile_rows)
    col_pos = lax.dynamic_slice_in_dim(coded, col_first, tile_cols)
    offset = jnp.clip(col_pos[None, :] - row_pos[:, None], -RELPOS_MAX, RELPOS_MAX) + RELPOS_MAX + 1
    both_live = (row_pos[:, None] >= 0) & (col_pos[None, :] >= 0)
    bin_index = jnp.where(both_live, offset, 0)
    table_rows = position_table.shape[0]
    padded_rows = (table_rows + 127) // 128 * 128
    table_padded = jnp.pad(position_table, ((0, padded_rows - table_rows), (0, 0)))
    one_hot = (
        bin_index.reshape(-1, 1) == jnp.arange(padded_rows, dtype=jnp.int32)[None, :]
    ).astype(jnp.bfloat16)
    pair_now = pair_state.astype(jnp.float32) + jnp.dot(
        one_hot, table_padded, preferred_element_type=jnp.float32
    ).reshape(tile_rows, tile_cols, channels)
    pair_flat = pair_now.reshape(-1, channels)
    bias_weight_t = jnp.swapaxes(bias_weight, 1, 2)
    live_column = residue_mask.reshape(-1, 1)
    bin_count = distance_weight.shape[1]
    bins_pair = jnp.stack(
        [
            jnp.pad(distance_weight, ((0, 0), (0, bin_count))),
            jnp.pad(distance_weight, ((0, 0), (bin_count, 0))),
        ]
    )
    layers = query_weight.shape[0]
    extra = bias_step(0, pair_flat, tile_rows, tile_cols, bias_norm_gain, bias_weight_t)
    seq_now, seq_all = seq_state, None
    for layer in range(layers):
        seq_now, seq_all, left, right = sequence_step(
            layer,
            seq_now,
            seq_all,
            extra,
            live_column,
            (attention_gain, outer_gain),
            (query_weight, key_weight, value_weight, gate_weight, out_weight),
            outer_weight,
            layer,
        )
        mats = (outer_out_weight, up_weight, down_weight)
        if layer < layers - 1:
            pair_flat, extra = pair_step(
                layer,
                pair_flat,
                left,
                right,
                tile_rows,
                tile_cols,
                mats,
                (transition_gain, bias_norm_gain),
                bias_weight_t,
            )
    distogram = last_step(
        layers - 1,
        pair_flat,
        left,
        right,
        tile_rows,
        tile_cols,
        mats,
        transition_gain,
        bins_pair,
        layers,
    )
    return (distogram, seq_now)


def solution(mesh):
    in_specs = (
        P("row", "col", None),
        P("row", "col"),
        P(),
        P(),
        P(),
        P(),
        P(),
        P(None, None, "col"),
        P(None, None, "col"),
        P(None, None, "col"),
        P(None, None, "col"),
        P(None, None, "col"),
        P(),
        P(),
        P(),
        P(),
        P(),
        P(),
        P(),
        P(),
    )
    out_specs = (P("row", "col", None), P("row", "col"))
    return jax.shard_map(
        per_device, mesh=mesh, in_specs=in_specs, out_specs=out_specs, check_vma=False
    )
```

profile of v0, /device:TPU:5, one launch (start us, length us, event | category | flops | bytes accessed | tf_op | source)
XLA Modules:
  0.0 116.8 jit_solution(9656457579083795430)
XLA Ops:
  0.6 0.0 copy-start
  0.6 0.8 compare_select_fusion
  1.4 0.1 broadcast_compare_fusion
  1.5 0.1 broadcast_compare_fusion.1
  1.6 0.1 add_select_fusion
  1.7 0.1 select_n.25
  1.8 1.5 %fusion = f32[4608,128]{1,0:T(8,128)S(1)} fusion(s32[4608]{0:T(1024)S(1)} %select_n.25, bf16[66,128]{1,0:T(8,128)(2,1)} %param.24), kind=kOutput, calls=%fused_computation.2 | convolution fusion | flops 151584768 | bytes 2394624 | tf_op jit(solution)/shard_map/dot_general | solution.py:599
  3.3 0.0 copy-done
  3.3 1.7 %convert_add_fusion = f32[96,48,128]{2,1,0:T(8,128)} fusion(f32[96,48,128]{2,1,0:T(8,128)S(1)} %bitcast.9, bf16[96,48,128]{2,1,0:T(8,128)(2,1)S(1)} %copy-done), kind=kLoop, calls=%fused_computation.1 | loop fusion | flops 1179648 | bytes 5898240 | tf_op jit(solution)/shard_map/add | solution.py:599
  5.0 0.0 copy-start.3
  5.0 5.2 %shard_map.203.refs_1_ = bf16[32,48,128]{2,1,0:T(8,128)(2,1)} custom-call(f32[4608,128]{1,0:T(8,128)} %bitcast.7, f32[2,128]{1,0:T(2,128)} %bias_gain_ref.1, bf16[2,32,128]{2,1,0:T(8,128)(2,1)} %bitcast.10), custom_call_target="tpu_custom_call" | custom-call | tf_op jit(solution)/shard_map/pallas_call | solution.py:268
  10.2 0.0 copy-done.3
  10.2 0.8 reshape.61.refs_2_.refs_3_
  11.0 28.9 %shard_map.204 = (bf16[96,128]{1,0:T(8,128)(2,1)}, bf16[8,96,128]{2,1,0:T(8,128)(2,1)}, bf16[96,128]{1,0:T(8,128)(2,1)}, bf16[48,128]{1,0:T(8,128)(2,1)}) custom-call(bf16[96,128]{1,0:T(8,128)(2,1)} %refs_0_.1, bf16[32,48,128]{2,1,0:T(8,128)(2,1)} %shard_map.203.refs_1_, s32[384,1]{1,0:T(8,128)} %reshape.61.refs_2_.refs_3_, f32[2,1024]{1,0:T(2,128)} %refs_4_.3, ...), custom_call_target="tpu_custom_call" | custom-call | tf_op jit(solution)/shard_map/pallas_call | solution.py:219
  40.0 13.3 %shard_map.205 = (bf16[4608,128]{1,0:T(8,128)(2,1)}, bf16[32,48,128]{2,1,0:T(8,128)(2,1)}) custom-call(f32[4608,128]{1,0:T(8,128)} %bitcast.8, bf16[96,128]{1,0:T(8,128)(2,1)} %get-tuple-element.11.left_ref, bf16[48,128]{1,0:T(8,128)(2,1)} %get-tuple-element.12.right_ref, bf16[2,128,128]{2,1,0:T(8,128)(2,1)} %outer_ref.3, bf16[2,128,512]{2,1,0:T(8,128)(2,1)} %up_ref.3, ...), custom_call_target="tpu_custom_call" | custom-call | tf_op jit(solution)/shard_map/pallas_call | solution.py:353
  53.3 0.0 copy-start.2
  53.3 23.8 %shard_map.206 = (bf16[96,128]{1,0:T(8,128)(2,1)}, bf16[8,96,128]{2,1,0:T(8,128)(2,1)}, bf16[96,128]{1,0:T(8,128)(2,1)}, bf16[48,128]{1,0:T(8,128)(2,1)}) custom-call(bf16[96,128]{1,0:T(8,128)(2,1)} %get-tuple-element.14.refs_0_, bf16[8,96,128]{2,1,0:T(8,128)(2,1)} %get-tuple-element.15.refs_1_, bf16[32,48,128]{2,1,0:T(8,128)(2,1)} %get-tuple-element.16.refs_2_, ...), custom_call_target="tpu_custom_call" | custom-call | tf_op jit(solution)/shard_map/pallas_call | solution.py:219
  77.1 0.0 copy-done.2
  77.1 0.1 copy.27
  77.3 0.1 pad_bitcast_fusion.1
  77.4 0.6 pad_maximum_fusion.bins_ref
  78.0 0.0 copy-start.1
  78.0 35.7 %shard_map.207 = bf16[96,48,64]{2,1,0:T(8,128)(2,1)} custom-call(bf16[4608,128]{1,0:T(8,128)(2,1)} %get-tuple-element.13.pair_ref, bf16[96,128]{1,0:T(8,128)(2,1)} %get-tuple-element.17.left_ref, bf16[48,128]{1,0:T(8,128)(2,1)} %get-tuple-element.18.right_ref, bf16[2,128,128]{2,1,0:T(8,128)(2,1)} %outer_ref.3, bf16[2,128,512]{2,1,0:T(8,128)(2,1)} %up_ref.3, ...), custom_call_target="tpu_custom_call" | custom-call | tf_op jit(solution)/shard_map/pallas_call | solution.py:535
  113.7 2.4 %copy.29 = bf16[96,48,64]{0,2,1:T(8,128)(2,1)} copy(bf16[96,48,64]{2,1,0:T(8,128)(2,1)} %shard_map.207) | data formatting | bytes 1179648
  116.2 0.0 copy-done.1
  116.2 0.6 copy.31
Async XLA Ops:
  0.6 2.7 %copy-start = (bf16[96,48,128]{2,1,0:T(8,128)(2,1)S(1)}, bf16[96,48,128]{2,1,0:T(8,128)(2,1)}, u32[]{:S(2)}) copy-start(bf16[96,48,128]{2,1,0:T(8,128)(2,1)} %param.20) | copy-start | bytes 3538948
  5.0 5.2 %copy-start.3 = (s32[384]{0:T(512)S(1)}, s32[384]{0:T(512)}, u32[]{:S(2)}) copy-start(s32[384]{0:T(512)} %param.23) | copy-start | bytes 4612
  53.3 23.8 %copy-start.2 = (bf16[128,64]{0,1:T(8,128)(2,1)S(1)}, bf16[128,64]{0,1:T(8,128)(2,1)}, u32[]{:S(2)}) copy-start(bf16[128,64]{0,1:T(8,128)(2,1)} %param.39) | copy-start | bytes 49156
  78.0 38.2 %copy-start.1 = (bf16[96,128]{1,0:T(8,128)(2,1)S(1)}, bf16[96,128]{1,0:T(8,128)(2,1)}, u32[]{:S(2)}) copy-start(bf16[96,128]{1,0:T(8,128)(2,1)} %get-tuple-element.33) | copy-start | bytes 73732
where the time goes:
time: 119 us; the launch traced here: 117 us
  Pallas kernels  107 us (90%)
  local copies, waits for them, and re-layouts  4.15 us (3%)
  other arithmetic  3.42 us (3%)
  matrix products  1.51 us (1%)
    pallas_call x2, Pallas kernels, sequence_step(): pl.pallas_call(kernel, out_shape=(jax.ShapeDtypeStruct((tr, width), bf16)...  52.8 us
    pallas_call x1, Pallas kernels, last_step(): pl.pallas_call(kernel, out_shape=jax.ShapeDtypeStruct((tile_rows, tile_co...  35.7 us
    pallas_call x1, Pallas kernels, pair_step(): pl.pallas_call(kernel, out_shape=(jax.ShapeDtypeStruct((tr * tc, channels...  13.3 us
    pallas_call x1, Pallas kernels, bias_step(): pl.pallas_call(kernel, out_shape=jax.ShapeDtypeStruct((heads, tc, lanes),...  5.18 us
    unnamed x11, local copies, waits for them, and re-layouts  3.19 us

commit v1 on v0

v1 whole, which is shorter than its diff:
```python
import jax
import jax.numpy as jnp
from jax import lax
from jax.experimental import pallas as pl
from jax.experimental.pallas import tpu as pltpu
from jax.sharding import PartitionSpec as P

HEAD_DIM = 32
RELPOS_MAX = 32
MESH = pl.DeviceIdType.MESH
OWN = 16


def normalize(values, weight_gain):
    average = jnp.mean(values, axis=-1, keepdims=True)
    centred = values - average
    spread = jnp.mean(centred * centred, axis=-1, keepdims=True)
    return centred * lax.rsqrt(spread + 1e-05) * weight_gain


def full_spec():
    return pl.BlockSpec(memory_space=pltpu.VMEM)


def any_spec():
    return pl.BlockSpec(memory_space=pl.ANY)


def remote(source, target, send, recv, where):
    return pltpu.make_async_remote_copy(
        src_ref=source,
        dst_ref=target,
        send_sem=send,
        recv_sem=recv,
        device_id=where,
        device_id_type=MESH,
    )


def settle(ref, sem):
    pltpu.make_async_copy(ref, ref, sem).wait()


def rows_at(start, size, step):
    return pl.ds(pl.multiple_of(start, step), size)


def trunk(pair_state, seq_tile, index_row, mask_row, table, gains, bias_weight_t, dist_t, mats):
    nr, nc = lax.axis_size("row"), lax.axis_size("col")
    tr, tc, ch = pair_state.shape
    width = seq_tile.shape[1]
    layers, cs = mats[0].shape[:2]
    heads = bias_weight_t.shape[1]
    hl = heads // nc
    length = nr * tr
    lanes = (tr + 127) // 128 * 128
    owners, per, parts = tr // OWN, tc // OWN, tr // tc
    chunks, half = tc // OWN, OWN // 2
    wide = mats[5].shape[2]
    bins = dist_t.shape[0]
    packed_rows = half * tc
    depth = packed_rows // nc
    score_scale = HEAD_DIM ** (-0.5)
    f32, bf16 = jnp.float32, jnp.bfloat16

    def kernel(*refs):
        it = iter(refs)
        pair_hbm, seq_ref, index_ref, mask_ref, table_ref = (next(it) for _ in range(5))
        att_gain, bias_gain, outer_gain, trans_gain = (next(it) for _ in range(4))
        bias_w, dist_ref = (next(it) for _ in range(2))
        q_hbm, k_hbm, v_hbm, g_hbm, out_hbm = (next(it) for _ in range(5))
        late_hbm = [next(it) for _ in range(4)]
        final_ref, seq_out = (next(it) for _ in range(2))
        q_w, k_w, v_w, g_w = (next(it) for _ in range(4))
        late_refs = [next(it) for _ in range(4)]
        outer_w, mix_w, up_w, down_w = late_refs
        pair_in, natural, pair_s, mixed, place, table_s, bins_s = (next(it) for _ in range(7))
        gathered, kv_all, bias_out, bias_all, query_s, gate_s = (next(it) for _ in range(6))
        wrow, stage, rs_recv, new_rows, lr_s, left_all, right_all = (next(it) for _ in range(7))
        left_dup, right_rep, seq_next, out_stage = (next(it) for _ in range(4))
        fresh_s, own_s, flat, spread_s, moved, landed, unpacked = (next(it) for _ in range(7))
        load_sem, seq_sem, w_sem, bias_send, bias_recv, kv_sem = (next(it) for _ in range(6))
        rs_sem, left_sem, right_sem, next_sem, out_sem = (next(it) for _ in range(5))
        one_sem, two_sem, three_sem = (next(it) for _ in range(3))

        row, col = lax.axis_index("row"), lax.axis_index("col")
        owner = jnp.minimum(col, owners - 1)
        holder, part_at = lax.div(col, parts), lax.rem(col, parts)

        pair_load = pltpu.make_async_copy(pair_hbm, pair_in, load_sem.at[0])
        pair_load.start()
        loads = [
            pltpu.make_async_copy(src, dst, load_sem.at[1 + n])
            for n, (src, dst) in enumerate(
                zip([k_hbm, v_hbm, q_hbm, g_hbm, *late_hbm], [k_w, v_w, q_w, g_w, *late_refs])
            )
        ]
        for load in loads:
            load.start()

        barrier = pltpu.get_barrier_semaphore()
        for step in range(1, nc):
            pl.semaphore_signal(
                barrier, inc=1, device_id={"col": lax.rem(col + step, nc)}, device_id_type=MESH
            )
        for step in range(1, nr):
            pl.semaphore_signal(
                barrier, inc=1, device_id={"row": lax.rem(row + step, nr)}, device_id_type=MESH
            )

        @pl.when(row != holder)
        def _():
            for slot in range(per):
                pl.semaphore_signal(
                    barrier,
                    inc=1,
                    device_id={"row": holder, "col": part_at * per + slot},
                    device_id_type=MESH,
                )

        is_owner = col < owners

        @pl.when(is_owner)
        def _():
            pl.semaphore_wait(barrier, nc + 2 * nr - 3)

        @pl.when(jnp.logical_not(is_owner))
        def _():
            pl.semaphore_wait(barrier, nc + nr - 2)

        for step in range(1, nc):
            remote(
                seq_ref,
                gathered.at[col],
                seq_sem.at[0],
                seq_sem.at[1],
                {"col": lax.rem(col + step, nc)},
            ).start()
        gathered[col] = seq_ref[...]
        for step in range(1, nc):
            peer = lax.rem(col + step, nc)
            remote(
                out_hbm.at[:, rows_at(peer * width, width, width), :],
                wrow.at[col],
                w_sem.at[0],
                w_sem.at[1],
                {"col": peer},
            ).start()
        own_w = pltpu.make_async_copy(
            out_hbm.at[:, rows_at(col * width, width, width), :], wrow.at[col], w_sem.at[2]
        )
        own_w.start()

        coded = jnp.where(mask_ref[...] > 0, index_ref[...], -1).astype(f32)
        for block in range(length // 128):
            line = coded[:, block * 128 : (block + 1) * 128]
            place[block * 128 : (block + 1) * 128, :] = jnp.broadcast_to(line, (128, 128)).T
        table_s[...] = jnp.zeros_like(table_s)
        table_s[0 : table_ref.shape[0], :] = table_ref[...].astype(f32)
        table_rows = table_s[...].astype(bf16)
        bins_s[...] = jnp.zeros_like(bins_s)
        bins_s[0:bins, 0:ch] = dist_ref[...]
        bins_s[bins : 2 * bins, ch : 2 * ch] = dist_ref[...]
        lane = lax.broadcasted_iota(jnp.int32, (1, ch), 1).astype(f32)
        low = lax.broadcasted_iota(jnp.int32, (1, ch), 1) < ch // 2

        def bias_of(layer, normed, at):
            mixed[pl.ds(pl.multiple_of(at * heads, heads), heads), 0:tr] = lax.dot_general(
                bias_w[layer], normed, (((1,), (1,)), ((), ())), preferred_element_type=f32
            )

        def send_bias(layer, k):
            span = pl.ds(k * OWN, OWN)
            for head in range(heads):
                bias_out[layer, head, k * OWN : (k + 1) * OWN, :] = mixed[
                    pl.ds(head, OWN, stride=heads), :
                ].astype(bf16)
            for step in range(1, nc):
                peer = lax.rem(col + step, nc)
                remote(
                    bias_out.at[layer, pl.ds(peer * hl, hl), span],
                    bias_all.at[layer, col, :, span],
                    bias_send.at[layer, k],
                    bias_recv.at[layer, k],
                    {"col": peer},
                ).start()
            bias_all[layer, col, :, k * OWN : (k + 1) * OWN, :] = bias_out[
                layer, pl.ds(col * hl, hl), k * OWN : (k + 1) * OWN, :
            ]

        def enter(k):
            natural[...] = (
                pair_in[:, k * OWN : (k + 1) * OWN, :].reshape(tr * OWN, ch).astype(f32)
            )

            @pl.loop(0, OWN, unroll=8)
            def _(j):
                row_pos = place[rows_at(row * tr, tr, 8), :]
                col_pos = place[pl.ds(col * tc + k * OWN + j, 1), :]
                offset = jnp.clip(col_pos - row_pos, -RELPOS_MAX, RELPOS_MAX) + (RELPOS_MAX + 1)
                live = (row_pos >= 0) & (col_pos >= 0)
                position = jnp.where(live, offset, 0.0)
                one_hot = jnp.where(position == lane, 1.0, 0.0).astype(bf16)
                value = natural[pl.ds(j, tr, stride=OWN), :] + jnp.dot(
                    one_hot, table_rows, preferred_element_type=f32
                )
                pair_s[rows_at((k * OWN + j) * tr, tr, 8), :] = value
                bias_of(0, normalize(value, bias_gain[0:1, :]).astype(bf16), j)

            send_bias(0, k)

        def project(layer, entering):
            normed = normalize(entering, att_gain[layer : layer + 1, :]).astype(bf16)

            def product(weight):
                return jnp.dot(normed, weight[layer], preferred_element_type=f32)

            if layer == 0:
                loads[0].wait()
            kv_all[layer, row, 0] = product(k_w).astype(bf16)
            if layer == 0:
                loads[1].wait()
            kv_all[layer, row, 1] = product(v_w).astype(bf16)
            for step in range(1, nr):
                remote(
                    kv_all.at[layer, row],
                    kv_all.at[layer, row],
                    kv_sem.at[layer, 0],
                    kv_sem.at[layer, 1],
                    {"row": lax.rem(row + step, nr)},
                ).start()
            if layer == 0:
                loads[2].wait()
            query_s[...] = (product(q_w) * score_scale).astype(bf16)
            if layer == 0:
                loads[3].wait()
            gate_s[...] = jax.nn.sigmoid(product(g_w))

        def attend(layer):
            settle(kv_all.at[layer, pl.ds(0, nr - 1)], kv_sem.at[layer, 1])
            for k in range(chunks):
                settle(
                    bias_all.at[layer, pl.ds(0, nc - 1), :, pl.ds(k * OWN, OWN)],
                    bias_recv.at[layer, k],
                )
            keys = kv_all[layer, :, 0].reshape(length, width)
            values = kv_all[layer, :, 1].reshape(length, width)
            live = place[:, 0:tr] >= 0
            head_of = lax.broadcasted_iota(jnp.int32, (tr, width), 1) // HEAD_DIM
            queries = query_s[...].astype(f32)
            attended = jnp.zeros((tr, width), f32)
            for head in range(hl):
                own = head_of == head
                query = jnp.where(own, queries, 0.0).astype(bf16)
                scores = lax.dot_general(
                    keys, query, (((1,), (1,)), ((), ())), preferred_element_type=f32
                )
                bias = bias_all[layer, :, head].reshape(length, lanes)[:, :tr]
                scores = jnp.where(live, scores + bias.astype(f32), -jnp.inf)
                shifted = jnp.exp(scores - jnp.max(scores, axis=0, keepdims=True))
                share = (shifted / jnp.sum(shifted, axis=0, keepdims=True)).astype(bf16)
                mixture = lax.dot_general(
                    share, values, (((0,), (0,)), ((), ())), preferred_element_type=f32
                )
                attended = jnp.where(own, mixture, attended)
            gated = (gate_s[...] * attended).astype(bf16)
            if layer == 0:
                own_w.wait()
                settle(wrow.at[pl.ds(0, nc - 1)], w_sem.at[1])
            weight = jnp.concatenate([wrow[p, layer] for p in range(nc)], axis=1)
            partial = jnp.dot(gated, weight, preferred_element_type=f32)
            stage[layer] = partial.reshape(owners, OWN, cs).astype(bf16)
            for step in range(owners):
                peer = lax.rem(col + step, owners)

                @pl.when(peer != col)
                def _(peer=peer):
                    remote(
                        stage.at[layer, peer],
                        rs_recv.at[layer, col],
                        rs_sem.at[layer, 0],
                        rs_sem.at[layer, 1],
                        {"col": peer},
                    ).start()

        def finish_rows(layer):
            at = rows_at(owner * OWN, OWN, OWN)

            @pl.when(is_owner)
            def _():
                rs_recv[layer, col] = stage[layer, owner]
                if layer == 0:
                    before = jnp.concatenate([gathered[p, at, :] for p in range(nc)], axis=1)
                else:
                    before = seq_next[at, :]
                total = before.astype(f32)
                settle(rs_recv.at[layer, pl.ds(0, nc - 1)], rs_sem.at[layer, 1])
                for p in range(nc):
                    total += rs_recv[layer, p].astype(f32)
                fresh = total.astype(bf16)
                new_rows[layer] = fresh
                outer_in = normalize(fresh.astype(f32), outer_gain[layer : layer + 1, :])
                lr_s[layer] = jnp.dot(
                    outer_in.astype(bf16), outer_w[layer], preferred_element_type=f32
                ).astype(bf16)
                slot = rows_at(lax.rem(owner, per) * OWN, OWN, OWN)
                for step in range(1, nr):
                    remote(
                        lr_s.at[layer],
                        right_all.at[layer, slot],
                        right_sem.at[layer, 0],
                        right_sem.at[layer, 1],
                        {
                            "row": lax.rem(row + step, nr),
                            "col": parts * row + lax.div(owner, per),
                        },
                    ).start()
                for step in range(1, nc):
                    remote(
                        lr_s.at[layer],
                        left_all.at[layer, at],
                        left_sem.at[layer, 0],
                        left_sem.at[layer, 1],
                        {"col": lax.rem(col + step, nc)},
                    ).start()
                left_all[layer, at, :] = lr_s[layer]
                if layer < layers - 1:
                    for step in range(1, nc):
                        remote(
                            new_rows.at[layer],
                            seq_next.at[at],
                            next_sem.at[0],
                            next_sem.at[1],
                            {"col": lax.rem(col + step, nc)},
                        ).start()
                    seq_next[at, :] = fresh
                else:
                    for p in range(nc):
                        out_stage[p] = fresh[:, p * width : (p + 1) * width]
                    for step in range(1, nc):
                        peer = lax.rem(col + step, nc)
                        remote(
                            out_stage.at[peer],
                            seq_out.at[at],
                            out_sem.at[0],
                            out_sem.at[1],
                            {"col": peer},
                        ).start()
                    seq_out[at, :] = out_stage[col]

        def from_owners(whole, most, sem):
            pl.when(is_owner)(lambda: settle(most, sem))
            pl.when(jnp.logical_not(is_owner))(lambda: settle(whole, sem))

        some = pl.ds(0, (owners - 1) * OWN)

        def sides(layer):
            from_owners(left_all.at[layer], left_all.at[layer, some], left_sem.at[layer, 1])

            @pl.when(row != holder)
            def _():
                settle(right_all.at[layer], right_sem.at[layer, 1])

            @pl.when(row == holder)
            def _():
                right_all[layer] = left_all[layer, rows_at(part_at * tc, tc, OWN), :]

            left = left_all[layer].astype(f32)
            left_dup[...] = jnp.where(low, left, pltpu.roll(left, ch // 2, axis=1))
            right = right_all[layer].astype(f32)
            right = jnp.where(low, pltpu.roll(right, ch // 2, axis=1), right)
            right_rep[...] = jnp.broadcast_to(right[:, None, :], (tc, 8, ch))

        group = 4

        def update(layer, k):
            last = layer == layers - 1
            trans = trans_gain[layer : layer + 1, :]

            @pl.loop(0, OWN // group, unroll=2)
            def _(step):
                j = pl.multiple_of(step * group, group) + k * OWN
                at = rows_at(j * tr, group * tr, 8)
                right = right_rep[pl.ds(j, group)][:, None]
                left = left_dup[...].reshape(1, tr // 8, 8, ch)
                features = jnp.where(low.reshape(1, 1, 1, ch), left * right, left - right)
                features = features.reshape(group * tr, ch).astype(bf16)
                middle = pair_s[at, :] + jnp.dot(
                    features, mix_w[layer], preferred_element_type=f32
                )
                normed = normalize(middle, trans).astype(bf16)
                hidden = jnp.maximum(
                    jnp.dot(normed, up_w[layer], preferred_element_type=f32), 0.0
                ).astype(bf16)
                fresh = (
                    middle + jnp.dot(hidden, down_w[layer], preferred_element_type=f32)
                ).astype(bf16)
                if last:
                    fresh_s[pl.ds(step * group, group)] = fresh.reshape(group, parts, tc, ch)
                else:
                    value = fresh.astype(f32)
                    pair_s[at, :] = value
                    normed = normalize(value, bias_gain[layer + 1 : layer + 2, :]).astype(bf16)
                    for n in range(group):
                        bias_of(layer + 1, normed[n * tr : (n + 1) * tr], step * group + n)

        def logits(k):
            for s in range(parts):
                both = jnp.concatenate(
                    [
                        fresh_s[0:half, s].reshape(packed_rows, ch),
                        fresh_s[half:OWN, s].reshape(packed_rows, ch),
                    ],
                    axis=1,
                )
                packed = lax.dot_general(
                    both, bins_s[...], (((1,), (1,)), ((), ())), preferred_element_type=f32
                )
                own_s[k, s] = packed
                rounded = packed.astype(bf16)
                for p in range(nc):
                    flat[k, p, s] = rounded[p * depth : (p + 1) * depth]
            for step in range(1, nc):
                peer = lax.rem(col + step, nc)
                remote(
                    flat.at[k, peer],
                    spread_s.at[k, col],
                    one_sem.at[k, 0],
                    one_sem.at[k, 1],
                    {"col": peer},
                ).start()

        def across(k):
            settle(spread_s.at[k, pl.ds(0, nc - 1)], one_sem.at[k, 1])
            for step in range(nc):
                origin = lax.rem(col + step, nc)
                peer, slot = lax.div(origin, parts), lax.rem(origin, parts)
                source = spread_s.at[k, origin] if step else flat.at[k, col]
                target = moved.at[k, row, slot]

                @pl.when(peer != row)
                def _(source=source, target=target, peer=peer):
                    remote(
                        source, target, two_sem.at[k, 0], two_sem.at[k, 1], {"row": peer}
                    ).start()

                @pl.when(peer == row)
                def _(source=source, target=target):
                    pltpu.make_async_copy(source, target, two_sem.at[k, 1]).start()

        def home(k):
            settle(moved.at[k], two_sem.at[k, 1])
            for step in range(nr):
                origin = lax.rem(row + step, nr)
                for s in range(parts):
                    peer = origin * parts + s
                    for slot in range(parts):
                        source = moved.at[k, origin, slot, s]
                        target = landed.at[k, slot, col]

                        @pl.when(peer != col)
                        def _(source=source, target=target, peer=peer):
                            remote(
                                source,
                                target,
                                three_sem.at[k, 0],
                                three_sem.at[k, 1],
                                {"col": peer},
                            ).start()

                        @pl.when(peer == col)
                        def _(source=source, target=target):
                            pltpu.make_async_copy(source, target, three_sem.at[k, 1]).start()

        def combine(k):
            settle(landed.at[k], three_sem.at[k, 1])
            for slot in range(parts):
                for p in range(nc):
                    unpacked[slot, p * depth : (p + 1) * depth, :] = landed[k, slot, p].astype(f32)

                @pl.loop(0, half, unroll=4)
                def _(n, slot=slot):
                    near = unpacked[slot, rows_at(n * tc, tc, 8), :]
                    far = pltpu.roll(near, bins, axis=1)
                    for other, at in ((near, n), (far, n + half)):
                        at = at + k * OWN
                        pieces = []
                        for c in range(chunks):
                            own = own_s[c, slot, pl.ds(at, half, stride=tc), :]
                            pieces += [own, pltpu.roll(own, bins, axis=1)]
                        total = (jnp.concatenate(pieces, axis=0) + other) * 0.5
                        final_ref[slot * tc + at] = total.astype(bf16)[:, :bins]

        pair_load.wait()
        for k in range(chunks):
            enter(k)
        settle(gathered.at[pl.ds(0, nc - 1)], seq_sem.at[1])
        project(0, jnp.concatenate([gathered[p] for p in range(nc)], axis=1).astype(f32))
        for layer in range(layers):
            attend(layer)
            if layer == 0:
                for load in loads[4:]:
                    load.wait()
            finish_rows(layer)
            sides(layer)
            if layer < layers - 1:
                for k in range(chunks):
                    update(layer, k)
                    send_bias(layer + 1, k)
                    if k == 0:
                        from_owners(seq_next, seq_next.at[some], next_sem.at[1])
                        project(layer + 1, seq_next[...].astype(f32))
        for k in range(chunks):
            update(layers - 1, k)
            logits(k)
            if k >= 1:
                across(k - 1)
            if k >= 2:
                home(k - 2)
        across(chunks - 1)
        for k in range(max(chunks - 2, 0), chunks):
            home(k)
        for k in range(chunks):
            combine(k)
        from_owners(seq_out, seq_out.at[some], out_sem.at[1])

        settle(gathered.at[pl.ds(0, nc - 1)], seq_sem.at[0])
        settle(wrow.at[pl.ds(0, nc - 1)], w_sem.at[0])
        for layer in range(layers):
            for k in range(chunks):
                settle(
                    bias_out.at[layer, pl.ds(0, (nc - 1) * hl), pl.ds(k * OWN, OWN)],
                    bias_send.at[layer, k],
                )
            settle(kv_all.at[layer, pl.ds(0, nr - 1)], kv_sem.at[layer, 0])

            from_owners(
                stage.at[layer], stage.at[layer, pl.ds(0, owners - 1)], rs_sem.at[layer, 0]
            )

            @pl.when(is_owner)
            def _(layer=layer):
                settle(
                    rs_recv.at[layer, pl.ds(0, nr - 1), :, pl.ds(0, wide)],
                    right_sem.at[layer, 0],
                )
                settle(
                    rs_recv.at[layer, pl.ds(0, nc - 1), :, pl.ds(0, wide)],
                    left_sem.at[layer, 0],
                )
                if layer < layers - 1:
                    settle(rs_recv.at[layer, pl.ds(0, nc - 1)], next_sem.at[0])
                else:
                    settle(out_stage.at[pl.ds(0, nc - 1)], out_sem.at[0])

        for k in range(chunks):
            settle(flat.at[k, pl.ds(0, nc - 1)], one_sem.at[k, 0])
            settle(flat.at[k, pl.ds(0, nc - parts)], two_sem.at[k, 0])
            settle(landed.at[k, :, pl.ds(0, nc - 1)], three_sem.at[k, 0])

    operands = (
        pair_state, seq_tile, index_row, mask_row, table, *gains, bias_weight_t, dist_t, *mats,
    )
    vm, dma = pltpu.VMEM, pltpu.SemaphoreType.DMA
    scratch = (
        [vm((layers, cs, width), bf16)] * 4
        + [vm(m.shape, bf16) for m in mats[5:]]
        + [
            vm((tr, tc, ch), bf16),
            vm((tr * OWN, ch), f32),
            vm((tc * tr, ch), f32),
            vm((OWN * heads, lanes), f32),
            vm((length, 128), f32),
            vm(((table.shape[0] + 127) // 128 * 128, ch), f32),
            vm((2 * bins, 2 * ch), bf16),
            vm((nc, tr, width), bf16),
            vm((layers, nr, 2, tr, width), bf16),
            vm((layers, heads, tc, lanes), bf16),
            vm((layers, nc, hl, tc, lanes), bf16),
            vm((tr, width), bf16),
            vm((tr, width), f32),
            vm((nc, layers, width, width), bf16),
            vm((layers, owners, OWN, cs), bf16),
            vm((layers, nc, OWN, cs), bf16),
            vm((layers, OWN, cs), bf16),
            vm((layers, OWN, wide), bf16),
            vm((layers, tr, wide), bf16),
            vm((layers, tc, wide), bf16),
            vm((tr, ch), f32),
            vm((tc, 8, ch), f32),
            vm((tr, cs), bf16),
            vm((nc, OWN, width), bf16),
            vm((OWN, parts, tc, ch), bf16),
            vm((chunks, parts, packed_rows, 2 * bins), f32),
            vm((chunks, nc, parts, depth, 2 * bins), bf16),
            vm((chunks, nc, parts, depth, 2 * bins), bf16),
            vm((chunks, nr, parts, parts, depth, 2 * bins), bf16),
            vm((chunks, parts, nc, depth, 2 * bins), bf16),
            vm((parts, packed_rows, 2 * bins), f32),
            dma((9,)),
            dma((2,)),
            dma((3,)),
            dma((layers, chunks)),
            dma((layers, chunks)),
            dma((layers, 2)),
            dma((layers, 2)),
            dma((layers, 2)),
            dma((layers, 2)),
            dma((2,)),
            dma((2,)),
            dma((chunks, 2)),
            dma((chunks, 2)),
            dma((chunks, 2)),
        ]
    )
    return pl.pallas_call(
        kernel,
        out_shape=(
            jax.ShapeDtypeStruct((tr, tc, bins), bf16),
            jax.ShapeDtypeStruct((tr, width), bf16),
        ),
        in_specs=[any_spec()] + [full_spec()] * 10 + [any_spec()] * 9,
        out_specs=(full_spec(),) * 2,
        scratch_shapes=scratch,
        compiler_params=pltpu.CompilerParams(collective_id=0, has_side_effects=True),
    )(*operands)


def per_device(
    pair_state,
    seq_state,
    residue_index,
    residue_mask,
    position_table,
    attention_gain,
    bias_norm_gain,
    query_weight,
    key_weight,
    value_weight,
    gate_weight,
    out_weight,
    bias_weight,
    outer_gain,
    outer_weight,
    outer_out_weight,
    transition_gain,
    up_weight,
    down_weight,
    distance_weight,
):
    return trunk(
        pair_state,
        seq_state,
        residue_index.reshape(1, -1),
        residue_mask.reshape(1, -1),
        position_table,
        (attention_gain, bias_norm_gain, outer_gain, transition_gain),
        jnp.swapaxes(bias_weight, 1, 2),
        distance_weight.T,
        (
            query_weight,
            key_weight,
            value_weight,
            gate_weight,
            out_weight,
            outer_weight,
            outer_out_weight,
            up_weight,
            down_weight,
        ),
    )


def solution(mesh):
    heads_split = P(None, None, "col")
    in_specs = (
        (P("row", "col", None), P("row", "col"))
        + (P(),) * 5
        + (heads_split,) * 5
        + (P(),) * 8
    )
    out_specs = (P("row", "col", None), P("row", "col"))
    return jax.shard_map(
        per_device, mesh=mesh, in_specs=in_specs, out_specs=out_specs, check_vma=False
    )
```

time: 119 us -> 91.9 us (0.77)
  Pallas kernels: 107 us -> 84.1 us
  other arithmetic: 3.42 us -> 0 us
  matrix products: 1.51 us -> 0 us
  local copies, waits for them, and re-layouts: 4.15 us -> 5.55 us
    pallas_call x5 -> x1, Pallas kernels: 107 us -> 84.1 us  [trunk(): pl.pallas_call(kernel, out_shape=(jax.ShapeDtypeStruct((tr, tc, bins), bf...]
    unnamed x11 -> x3, local copies, waits for them, and re-layouts: 3.19 us -> 0.61 us
    pallas_call x0 -> x1, local copies, waits for them, and re-layouts: none -> 2.45 us  [trunk(): pl.pallas_call(kernel, out_shape=(jax.ShapeDtypeStruct((tr, tc, bins), bf...]
    add x1 -> x0, other arithmetic: 1.74 us -> none  [per_device(): pair_state.astype(jnp.float32)]
    reshape x1 -> x2, local copies, waits for them, and re-layouts: 0.79 us -> 2.49 us  [the longest x1 1.25 us: per_device(): residue_index.reshape(1, -1)]
    dot_general x1 -> x0, matrix products: 1.51 us -> none  [per_device(): jnp.dot(one_hot, table_padded, preferred_element_type=jnp.float32)]
where the time goes in v1:
time: 91.9 us; the launch traced here: 90.3 us
  Pallas kernels  84.1 us (92%)
  local copies, waits for them, and re-layouts  5.55 us (6%)
    pallas_call x1, Pallas kernels, trunk(): pl.pallas_call(kernel, out_shape=(jax.ShapeDtypeStruct((tr, tc, bins), bf...  84.1 us
    pallas_call x1, local copies, waits for them, and re-layouts, trunk(): pl.pallas_call(kernel, out_shape=(jax.ShapeDtypeStruct((tr, tc, bins), bf...  2.45 us

profile of v1, /device:TPU:5, one launch (start us, length us, event | category | flops | bytes accessed | tf_op | source)
XLA Modules:
  0.0 90.3 jit_solution(14787243506089837520)
XLA Ops:
  0.6 1.2 %reshape.10.refs_2_ = s32[1,384]{1,0:T(1,128)} reshape(s32[384]{0:T(512)} %param.22) | data formatting | bytes 3072 | tf_op jit(solution)/shard_map/reshape | solution.py:654
  1.9 1.2 %reshape.11.refs_3_ = s32[1,384]{1,0:T(1,128)} reshape(s32[384]{0:T(512)} %param.23) | data formatting | bytes 3072 | tf_op jit(solution)/shard_map/reshape | solution.py:655
  3.1 84.1 %shard_map.203 = (bf16[96,48,64]{2,1,0:T(8,128)(2,1)}, bf16[96,128]{1,0:T(8,128)(2,1)}) custom-call(bf16[96,48,128]{2,1,0:T(8,128)(2,1)} %refs_0_.1, bf16[96,128]{1,0:T(8,128)(2,1)} %refs_1_.1, s32[1,384]{1,0:T(1,128)} %reshape.10.refs_2_, s32[1,384]{1,0:T(1,128)} %reshape.11.refs_3_, bf16[66,128]{1,0:T(8,128)(2,1)} %refs_4_.1, f32[2,1024]{1,0:T(2,128)} %refs_5_.1, ...), custom_call_target="tpu_custom_call" | custom-call | tf_op jit(solution)/shard_map/pallas_call | solution.py:616
  87.2 0.0 copy-start
  87.2 2.4 %copy.22 = bf16[96,48,64]{0,2,1:T(8,128)(2,1)} copy(bf16[96,48,64]{2,1,0:T(8,128)(2,1)} %get-tuple-element.2) | data formatting | bytes 1179648 | tf_op jit(solution)/shard_map/pallas_call | solution.py:616
  89.7 0.0 copy-done
  89.7 0.6 copy.24
Async XLA Ops:
  87.2 2.5 %copy-start = (bf16[96,128]{1,0:T(8,128)(2,1)S(1)}, bf16[96,128]{1,0:T(8,128)(2,1)}, u32[]{:S(2)}) copy-start(bf16[96,128]{1,0:T(8,128)(2,1)} %get-tuple-element.7) | copy-start | bytes 73732

commit v2 on v1

--- a/solution.py
+++ b/solution.py
@@ -9,6 +9,8 @@
 RELPOS_MAX = 32
 MESH = pl.DeviceIdType.MESH
 OWN = 16
+PIECE = 8
+FAR = 1e6
 
 
 def normalize(values, weight_gain):
@@ -45,7 +47,7 @@
     return pl.ds(pl.multiple_of(start, step), size)
 
 
-def trunk(pair_state, seq_tile, index_row, mask_row, table, gains, bias_weight_t, dist_t, mats):
+def trunk(pair_state, seq_tile, index, mask, table, gains, bias_weight_t, dist_t, mats):
     nr, nc = lax.axis_size("row"), lax.axis_size("col")
     tr, tc, ch = pair_state.shape
     width = seq_tile.shape[1]
@@ -55,31 +57,35 @@
     length = nr * tr
     lanes = (tr + 127) // 128 * 128
     owners, per, parts = tr // OWN, tc // OWN, tr // tc
-    chunks, half = tc // OWN, OWN // 2
+    chunks, spans, half = tc // OWN, tc // PIECE, tc // 2
     wide = mats[5].shape[2]
     bins = dist_t.shape[0]
-    packed_rows = half * tc
+    packed_rows = PIECE * half
     depth = packed_rows // nc
     score_scale = HEAD_DIM ** (-0.5)
+    gap = OWN + 8
     f32, bf16 = jnp.float32, jnp.bfloat16
 
     def kernel(*refs):
         it = iter(refs)
-        pair_hbm, seq_ref, index_ref, mask_ref, table_ref = (next(it) for _ in range(5))
-        att_gain, bias_gain, outer_gain, trans_gain = (next(it) for _ in range(4))
-        bias_w, dist_ref = (next(it) for _ in range(2))
+        pair_hbm, seq_hbm = (next(it) for _ in range(2))
+        small_hbm = [next(it) for _ in range(9)]
         q_hbm, k_hbm, v_hbm, g_hbm, out_hbm = (next(it) for _ in range(5))
         late_hbm = [next(it) for _ in range(4)]
         final_ref, seq_out = (next(it) for _ in range(2))
+        small_refs = [next(it) for _ in range(9)]
+        index_ref, mask_ref, table_ref = small_refs[:3]
+        att_gain, bias_gain, outer_gain, trans_gain, bias_w, dist_ref = small_refs[3:]
         q_w, k_w, v_w, g_w = (next(it) for _ in range(4))
         late_refs = [next(it) for _ in range(4)]
         outer_w, mix_w, up_w, down_w = late_refs
         pair_in, natural, pair_s, mixed, place, table_s, bins_s = (next(it) for _ in range(7))
-        gathered, kv_all, bias_out, bias_all, query_s, gate_s = (next(it) for _ in range(6))
+        home_w, mirror_s, score_s = (next(it) for _ in range(3))
+        gathered, kv_all, bias_out, bias_all, query_s, gate_s, normed_s = (next(it) for _ in range(7))
         wrow, stage, rs_recv, new_rows, lr_s, left_all, right_all = (next(it) for _ in range(7))
         left_dup, right_rep, seq_next, out_stage = (next(it) for _ in range(4))
-        fresh_s, own_s, flat, spread_s, moved, landed, unpacked = (next(it) for _ in range(7))
-        load_sem, seq_sem, w_sem, bias_send, bias_recv, kv_sem = (next(it) for _ in range(6))
+        flat, spread_s, moved, landed, unpacked = (next(it) for _ in range(5))
+        load_sem, small_sem, seq_sem, w_sem, bias_send, bias_recv, kv_sem = (next(it) for _ in range(7))
         rs_sem, left_sem, right_sem, next_sem, out_sem = (next(it) for _ in range(5))
         one_sem, two_sem, three_sem = (next(it) for _ in range(3))
 
@@ -87,6 +93,32 @@
         owner = jnp.minimum(col, owners - 1)
         holder, part_at = lax.div(col, parts), lax.rem(col, parts)
 
+        barrier = pltpu.get_barrier_semaphore()
+        for step in range(1, nc):
+            pl.semaphore_signal(
+                barrier, inc=1, device_id={"col": lax.rem(col + step, nc)}, device_id_type=MESH
+            )
+        for step in range(1, nr):
+            pl.semaphore_signal(
+                barrier, inc=1, device_id={"row": lax.rem(row + step, nr)}, device_id_type=MESH
+            )
+
+        @pl.when(row != holder)
+        def _():
+            for slot in range(per):
+                pl.semaphore_signal(
+                    barrier,
+                    inc=1,
+                    device_id={"row": holder, "col": part_at * per + slot},
+                    device_id_type=MESH,
+                )
+
+        small = [
+            pltpu.make_async_copy(src, dst, small_sem.at[n])
+            for n, (src, dst) in enumerate(zip(small_hbm, small_refs))
+        ]
+        for load in small:
+            load.start()
         pair_load = pltpu.make_async_copy(pair_hbm, pair_in, load_sem.at[0])
         pair_load.start()
         loads = [
@@ -98,26 +130,6 @@
         for load in loads:
             load.start()
 
-        barrier = pltpu.get_barrier_semaphore()
-        for step in range(1, nc):
-            pl.semaphore_signal(
-                barrier, inc=1, device_id={"col": lax.rem(col + step, nc)}, device_id_type=MESH
-            )
-        for step in range(1, nr):
-            pl.semaphore_signal(
-                barrier, inc=1, device_id={"row": lax.rem(row + step, nr)}, device_id_type=MESH
-            )
-
-        @pl.when(row != holder)
-        def _():
-            for slot in range(per):
-                pl.semaphore_signal(
-                    barrier,
-                    inc=1,
-                    device_id={"row": holder, "col": part_at * per + slot},
-                    device_id_type=MESH,
-                )
-
         is_owner = col < owners
 
         @pl.when(is_owner)
@@ -130,28 +142,22 @@
 
         for step in range(1, nc):
             remote(
-                seq_ref,
+                seq_hbm,
                 gathered.at[col],
                 seq_sem.at[0],
                 seq_sem.at[1],
                 {"col": lax.rem(col + step, nc)},
             ).start()
-        gathered[col] = seq_ref[...]
-        for step in range(1, nc):
-            peer = lax.rem(col + step, nc)
-            remote(
-                out_hbm.at[:, rows_at(peer * width, width, width), :],
-                wrow.at[col],
-                w_sem.at[0],
-                w_sem.at[1],
-                {"col": peer},
-            ).start()
+        own_seq = pltpu.make_async_copy(seq_hbm, gathered.at[col], seq_sem.at[2])
+        own_seq.start()
         own_w = pltpu.make_async_copy(
             out_hbm.at[:, rows_at(col * width, width, width), :], wrow.at[col], w_sem.at[2]
         )
         own_w.start()
 
-        coded = jnp.where(mask_ref[...] > 0, index_ref[...], -1).astype(f32)
+        for load in small:
+            load.wait()
+        coded = jnp.where(mask_ref[...] > 0, index_ref[...].astype(f32), FAR).reshape(1, length)
         for block in range(length // 128):
             line = coded[:, block * 128 : (block + 1) * 128]
             place[block * 128 : (block + 1) * 128, :] = jnp.broadcast_to(line, (128, 128)).T
@@ -161,11 +167,22 @@
         bins_s[...] = jnp.zeros_like(bins_s)
         bins_s[0:bins, 0:ch] = dist_ref[...]
         bins_s[bins : 2 * bins, ch : 2 * ch] = dist_ref[...]
+        home_w[...] = jnp.zeros_like(home_w)
+        unit = lax.broadcasted_iota(jnp.int32, (bins, bins), 0) == lax.broadcasted_iota(
+            jnp.int32, (bins, bins), 1
+        )
+        unit = jnp.where(unit, 1.0, 0.0).astype(bf16)
+        for n in range(2):
+            home_w[n, :, 0:ch] = dist_ref[...]
+            home_w[n, :, ch + n * bins : ch + (n + 1) * bins] = unit
         lane = lax.broadcasted_iota(jnp.int32, (1, ch), 1).astype(f32)
+        shift = lane - (RELPOS_MAX + 1)
+        least = jnp.where(lane == 0, -4 * FAR, jnp.where(lane == 1, -FAR / 2, shift))
+        most = jnp.where(lane == 0, -FAR / 2, jnp.where(lane == 2 * RELPOS_MAX + 1, FAR, shift))
         low = lax.broadcasted_iota(jnp.int32, (1, ch), 1) < ch // 2
 
         def bias_of(layer, normed, at):
-            mixed[pl.ds(pl.multiple_of(at * heads, heads), heads), 0:tr] = lax.dot_general(
+            mixed[at * heads : (at + 1) * heads, 0:tr] = lax.dot_general(
                 bias_w[layer], normed, (((1,), (1,)), ((), ())), preferred_element_type=f32
             )
 
@@ -189,38 +206,48 @@
             ]
 
         def enter(k):
-            natural[...] = (
-                pair_in[:, k * OWN : (k + 1) * OWN, :].reshape(tr * OWN, ch).astype(f32)
-            )
-
-            @pl.loop(0, OWN, unroll=8)
-            def _(j):
-                row_pos = place[rows_at(row * tr, tr, 8), :]
+            for i in range(tr):
+                natural[i * gap : i * gap + OWN, :] = pair_in[
+                    i, k * OWN : (k + 1) * OWN, :
+                ].astype(f32)
+
+            row_pos = place[rows_at(row * tr, tr, 8), :]
+            hots = []
+            for j in range(OWN):
                 col_pos = place[pl.ds(col * tc + k * OWN + j, 1), :]
-                offset = jnp.clip(col_pos - row_pos, -RELPOS_MAX, RELPOS_MAX) + (RELPOS_MAX + 1)
-                live = (row_pos >= 0) & (col_pos >= 0)
-                position = jnp.where(live, offset, 0.0)
-                one_hot = jnp.where(position == lane, 1.0, 0.0).astype(bf16)
-                value = natural[pl.ds(j, tr, stride=OWN), :] + jnp.dot(
-                    one_hot, table_rows, preferred_element_type=f32
-                )
-                pair_s[rows_at((k * OWN + j) * tr, tr, 8), :] = value
-                bias_of(0, normalize(value, bias_gain[0:1, :]).astype(bf16), j)
-
+                col_pos = jnp.where(col_pos < FAR, col_pos, -FAR)
+                offset = col_pos - row_pos
+                hot = (offset >= least) & (offset <= most)
+                hots.append(jnp.where(hot, 1.0, 0.0).astype(bf16))
+            value = jnp.concatenate(
+                [natural[pl.ds(j, tr, stride=gap), :] for j in range(OWN)], axis=0
+            ) + jnp.dot(jnp.concatenate(hots, axis=0), table_rows, preferred_element_type=f32)
+            pair_s[k * OWN * tr : (k + 1) * OWN * tr, :] = value
+            normed = normalize(value, bias_gain[0:1, :]).astype(bf16)
+            for j in range(OWN):
+                bias_of(0, normed[j * tr : (j + 1) * tr], j)
             send_bias(0, k)
 
+        def swap_weights():
+            for step in range(1, nc):
+                peer = lax.rem(col + step, nc)
+                remote(
+                    out_hbm.at[:, rows_at(peer * width, width, width), :],
+                    wrow.at[col],
+                    w_sem.at[0],
+                    w_sem.at[1],
+                    {"col": peer},
+                ).start()
+
+        def product(layer, k, weight):
+            if layer == 0:
+                loads[k].wait()
+            return jnp.dot(normed_s[...], weight[layer], preferred_element_type=f32)
+
         def project(layer, entering):
-            normed = normalize(entering, att_gain[layer : layer + 1, :]).astype(bf16)
-
-            def product(weight):
-                return jnp.dot(normed, weight[layer], preferred_element_type=f32)
-
-            if layer == 0:
-                loads[0].wait()
-            kv_all[layer, row, 0] = product(k_w).astype(bf16)
-            if layer == 0:
-                loads[1].wait()
-            kv_all[layer, row, 1] = product(v_w).astype(bf16)
+            normed_s[...] = normalize(entering, att_gain[layer : layer + 1, :]).astype(bf16)
+            kv_all[layer, row, 0] = product(layer, 0, k_w).astype(bf16)
+            kv_all[layer, row, 1] = product(layer, 1, v_w).astype(bf16)
             for step in range(1, nr):
                 remote(
                     kv_all.at[layer, row],
@@ -229,36 +256,36 @@
                     kv_sem.at[layer, 1],
                     {"row": lax.rem(row + step, nr)},
                 ).start()
-            if layer == 0:
-                loads[2].wait()
-            query_s[...] = (product(q_w) * score_scale).astype(bf16)
-            if layer == 0:
-                loads[3].wait()
-            gate_s[...] = jax.nn.sigmoid(product(g_w))
+
+        def project_rest(layer):
+            query_s[...] = (product(layer, 2, q_w) * score_scale).astype(bf16)
+            gate_s[...] = jax.nn.sigmoid(product(layer, 3, g_w))
 
         def attend(layer):
             settle(kv_all.at[layer, pl.ds(0, nr - 1)], kv_sem.at[layer, 1])
+            keys = kv_all[layer, :, 0].reshape(length, width)
+            values = kv_all[layer, :, 1].reshape(length, width)
+            live = place[:, 0:tr] < FAR
+            head_of = lax.broadcasted_iota(jnp.int32, (tr, width), 1) // HEAD_DIM
+            queries = query_s[...].astype(f32)
+            attended = jnp.zeros((tr, width), f32)
+            for head in range(hl):
+                query = jnp.where(head_of == head, queries, 0.0).astype(bf16)
+                score_s[head, :, 0:tr] = lax.dot_general(
+                    keys, query, (((1,), (1,)), ((), ())), preferred_element_type=f32
+                )
             for k in range(chunks):
                 settle(
                     bias_all.at[layer, pl.ds(0, nc - 1), :, pl.ds(k * OWN, OWN)],
                     bias_recv.at[layer, k],
                 )
-            keys = kv_all[layer, :, 0].reshape(length, width)
-            values = kv_all[layer, :, 1].reshape(length, width)
-            live = place[:, 0:tr] >= 0
-            head_of = lax.broadcasted_iota(jnp.int32, (tr, width), 1) // HEAD_DIM
-            queries = query_s[...].astype(f32)
-            attended = jnp.zeros((tr, width), f32)
             for head in range(hl):
                 own = head_of == head
-                query = jnp.where(own, queries, 0.0).astype(bf16)
-                scores = lax.dot_general(
-                    keys, query, (((1,), (1,)), ((), ())), preferred_element_type=f32
-                )
+                scores = score_s[head, :, 0:tr]
                 bias = bias_all[layer, :, head].reshape(length, lanes)[:, :tr]
                 scores = jnp.where(live, scores + bias.astype(f32), -jnp.inf)
                 shifted = jnp.exp(scores - jnp.max(scores, axis=0, keepdims=True))
-                share = (shifted / jnp.sum(shifted, axis=0, keepdims=True)).astype(bf16)
+                share = (shifted * (1.0 / jnp.sum(shifted, axis=0, keepdims=True))).astype(bf16)
                 mixture = lax.dot_general(
                     share, values, (((0,), (0,)), ((), ())), preferred_element_type=f32
                 )
@@ -371,55 +398,47 @@
             right = jnp.where(low, pltpu.roll(right, ch // 2, axis=1), right)
             right_rep[...] = jnp.broadcast_to(right[:, None, :], (tc, 8, ch))
 
-        group = 4
-
-        def update(layer, k):
-            last = layer == layers - 1
-            trans = trans_gain[layer : layer + 1, :]
-
-            @pl.loop(0, OWN // group, unroll=2)
-            def _(step):
-                j = pl.multiple_of(step * group, group) + k * OWN
-                at = rows_at(j * tr, group * tr, 8)
-                right = right_rep[pl.ds(j, group)][:, None]
-                left = left_dup[...].reshape(1, tr // 8, 8, ch)
-                features = jnp.where(low.reshape(1, 1, 1, ch), left * right, left - right)
-                features = features.reshape(group * tr, ch).astype(bf16)
-                middle = pair_s[at, :] + jnp.dot(
-                    features, mix_w[layer], preferred_element_type=f32
-                )
-                normed = normalize(middle, trans).astype(bf16)
-                hidden = jnp.maximum(
-                    jnp.dot(normed, up_w[layer], preferred_element_type=f32), 0.0
-                ).astype(bf16)
-                fresh = (
-                    middle + jnp.dot(hidden, down_w[layer], preferred_element_type=f32)
-                ).astype(bf16)
-                if last:
-                    fresh_s[pl.ds(step * group, group)] = fresh.reshape(group, parts, tc, ch)
-                else:
-                    value = fresh.astype(f32)
-                    pair_s[at, :] = value
-                    normed = normalize(value, bias_gain[layer + 1 : layer + 2, :]).astype(bf16)
-                    for n in range(group):
-                        bias_of(layer + 1, normed[n * tr : (n + 1) * tr], step * group + n)
+        def update(layer, k, count):
+            at = slice(k * count * tr, (k + 1) * count * tr)
+            right = right_rep[k * count : (k + 1) * count][:, None]
+            left = left_dup[...].reshape(1, tr // 8, 8, ch)
+            features = jnp.where(low.reshape(1, 1, 1, ch), left * right, left - right)
+            features = features.reshape(count * tr, ch).astype(bf16)
+            middle = pair_s[at, :] + jnp.dot(features, mix_w[layer], preferred_element_type=f32)
+            normed = normalize(middle, trans_gain[layer : layer + 1, :]).astype(bf16)
+            hidden = jnp.maximum(
+                jnp.dot(normed, up_w[layer], preferred_element_type=f32), 0.0
+            ).astype(bf16)
+            fresh = (
+                middle + jnp.dot(hidden, down_w[layer], preferred_element_type=f32)
+            ).astype(bf16)
+            value = fresh.astype(f32)
+            pair_s[at, :] = value
+            if layer < layers - 1:
+                normed = normalize(value, bias_gain[layer + 1 : layer + 2, :]).astype(bf16)
+                for n in range(count):
+                    bias_of(layer + 1, normed[n * tr : (n + 1) * tr], n)
 
         def logits(k):
             for s in range(parts):
-                both = jnp.concatenate(
-                    [
-                        fresh_s[0:half, s].reshape(packed_rows, ch),
-                        fresh_s[half:OWN, s].reshape(packed_rows, ch),
-                    ],
-                    axis=1,
-                )
+                sides = [
+                    jnp.concatenate(
+                        [
+                            pair_s[pl.ds((k * PIECE + j) * tr + s * tc + n * half, half), :]
+                            for j in range(PIECE)
+                        ],
+                        axis=0,
+                    )
+                    for n in range(2)
+                ]
                 packed = lax.dot_general(
-                    both, bins_s[...], (((1,), (1,)), ((), ())), preferred_element_type=f32
-                )
-                own_s[k, s] = packed
-                rounded = packed.astype(bf16)
+                    jnp.concatenate(sides, axis=1).astype(bf16),
+                    bins_s[...],
+                    (((1,), (1,)), ((), ())),
+                    preferred_element_type=f32,
+                ).astype(bf16)
                 for p in range(nc):
-                    flat[k, p, s] = rounded[p * depth : (p + 1) * depth]
+                    flat[k, p, s] = packed[p * depth : (p + 1) * depth]
             for step in range(1, nc):
                 peer = lax.rem(col + step, nc)
                 remote(
@@ -472,30 +491,46 @@
                         def _(source=source, target=target):
                             pltpu.make_async_copy(source, target, three_sem.at[k, 1]).start()
 
-        def combine(k):
+        def collect(k):
             settle(landed.at[k], three_sem.at[k, 1])
             for slot in range(parts):
                 for p in range(nc):
-                    unpacked[slot, p * depth : (p + 1) * depth, :] = landed[k, slot, p].astype(f32)
-
-                @pl.loop(0, half, unroll=4)
-                def _(n, slot=slot):
-                    near = unpacked[slot, rows_at(n * tc, tc, 8), :]
-                    far = pltpu.roll(near, bins, axis=1)
-                    for other, at in ((near, n), (far, n + half)):
-                        at = at + k * OWN
-                        pieces = []
-                        for c in range(chunks):
-                            own = own_s[c, slot, pl.ds(at, half, stride=tc), :]
-                            pieces += [own, pltpu.roll(own, bins, axis=1)]
-                        total = (jnp.concatenate(pieces, axis=0) + other) * 0.5
-                        final_ref[slot * tc + at] = total.astype(bf16)[:, :bins]
+                    unpacked[k % 2, slot, p * depth : (p + 1) * depth, :] = landed[
+                        k, slot, p
+                    ].astype(f32)
+
+            @pl.loop(0, half, unroll=8)
+            def _(n):
+                for slot in range(parts):
+                    start = slot * tc + k * PIECE
+                    mirror_s[n, start : start + PIECE, :] = unpacked[
+                        k % 2, slot, pl.ds(n, PIECE, stride=half), :
+                    ]
+
+        def combine():
+            @pl.loop(0, half, unroll=4)
+            def _(n):
+                mirrored = mirror_s[n].astype(bf16)
+                for side in range(2):
+                    j = n + side * half
+                    own = pair_s[rows_at(j * tr, tr, 8), :].astype(bf16)
+                    total = lax.dot_general(
+                        home_w[side],
+                        jnp.concatenate([own, mirrored], axis=1),
+                        (((1,), (1,)), ((), ())),
+                        preferred_element_type=f32,
+                    )
+                    final_ref[j] = (total * 0.5).astype(bf16)
 
         pair_load.wait()
-        for k in range(chunks):
-            enter(k)
+        enter(0)
+        own_seq.wait()
         settle(gathered.at[pl.ds(0, nc - 1)], seq_sem.at[1])
         project(0, jnp.concatenate([gathered[p] for p in range(nc)], axis=1).astype(f32))
+        swap_weights()
+        for k in range(1, chunks):
+            enter(k)
+        project_rest(0)
         for layer in range(layers):
             attend(layer)
             if layer == 0:
@@ -505,23 +540,29 @@
             sides(layer)
             if layer < layers - 1:
                 for k in range(chunks):
-                    update(layer, k)
+                    update(layer, k, OWN)
                     send_bias(layer + 1, k)
                     if k == 0:
                         from_owners(seq_next, seq_next.at[some], next_sem.at[1])
                         project(layer + 1, seq_next[...].astype(f32))
-        for k in range(chunks):
-            update(layers - 1, k)
+                project_rest(layer + 1)
+        for k in range(spans):
+            update(layers - 1, k, PIECE)
             logits(k)
             if k >= 1:
                 across(k - 1)
+            if k >= 3:
+                home(k - 3)
+            if k >= 5:
+                collect(k - 5)
+        across(spans - 1)
+        for k in range(max(spans - 3, 0), spans):
+            home(k)
             if k >= 2:
-                home(k - 2)
-        across(chunks - 1)
-        for k in range(max(chunks - 2, 0), chunks):
-            home(k)
-        for k in range(chunks):
-            combine(k)
+                collect(k - 2)
+        for k in range(max(spans - 2, 0), spans):
+            collect(k)
+        combine()
         from_owners(seq_out, seq_out.at[some], out_sem.at[1])
 
         settle(gathered.at[pl.ds(0, nc - 1)], seq_sem.at[0])
@@ -553,32 +594,37 @@
                 else:
                     settle(out_stage.at[pl.ds(0, nc - 1)], out_sem.at[0])
 
-        for k in range(chunks):
+        for k in range(spans):
             settle(flat.at[k, pl.ds(0, nc - 1)], one_sem.at[k, 0])
             settle(flat.at[k, pl.ds(0, nc - parts)], two_sem.at[k, 0])
             settle(landed.at[k, :, pl.ds(0, nc - 1)], three_sem.at[k, 0])
 
     operands = (
-        pair_state, seq_tile, index_row, mask_row, table, *gains, bias_weight_t, dist_t, *mats,
+        pair_state, seq_tile, index, mask, table, *gains, bias_weight_t, dist_t, *mats,
     )
     vm, dma = pltpu.VMEM, pltpu.SemaphoreType.DMA
     scratch = (
-        [vm((layers, cs, width), bf16)] * 4
+        [vm(x.shape, x.dtype) for x in operands[2:11]]
+        + [vm((layers, cs, width), bf16)] * 4
         + [vm(m.shape, bf16) for m in mats[5:]]
         + [
             vm((tr, tc, ch), bf16),
-            vm((tr * OWN, ch), f32),
+            vm((tr * gap, ch), f32),
             vm((tc * tr, ch), f32),
             vm((OWN * heads, lanes), f32),
             vm((length, 128), f32),
             vm(((table.shape[0] + 127) // 128 * 128, ch), f32),
             vm((2 * bins, 2 * ch), bf16),
+            vm((2, bins, 2 * ch), bf16),
+            vm((half, tr, 2 * bins), f32),
+            vm((hl, length, lanes), f32),
             vm((nc, tr, width), bf16),
             vm((layers, nr, 2, tr, width), bf16),
             vm((layers, heads, tc, lanes), bf16),
             vm((layers, nc, hl, tc, lanes), bf16),
             vm((tr, width), bf16),
             vm((tr, width), f32),
+            vm((tr, cs), bf16),
             vm((nc, layers, width, width), bf16),
             vm((layers, owners, OWN, cs), bf16),
             vm((layers, nc, OWN, cs), bf16),
@@ -590,15 +636,14 @@
             vm((tc, 8, ch), f32),
             vm((tr, cs), bf16),
             vm((nc, OWN, width), bf16),
-            vm((OWN, parts, tc, ch), bf16),
-            vm((chunks, parts, packed_rows, 2 * bins), f32),
-            vm((chunks, nc, parts, depth, 2 * bins), bf16),
-            vm((chunks, nc, parts, depth, 2 * bins), bf16),
-            vm((chunks, nr, parts, parts, depth, 2 * bins), bf16),
-            vm((chunks, parts, nc, depth, 2 * bins), bf16),
-            vm((parts, packed_rows, 2 * bins), f32),
+            vm((spans, nc, parts, depth, 2 * bins), bf16),
+            vm((spans, nc, parts, depth, 2 * bins), bf16),
+            vm((spans, nr, parts, parts, depth, 2 * bins), bf16),
+            vm((spans, parts, nc, depth, 2 * bins), bf16),
+            vm((2, parts, packed_rows, 2 * bins), f32),
             dma((9,)),
-            dma((2,)),
+            dma((9,)),
+            dma((3,)),
             dma((3,)),
             dma((layers, chunks)),
             dma((layers, chunks)),
@@ -608,22 +653,60 @@
             dma((layers, 2)),
             dma((2,)),
             dma((2,)),
-            dma((chunks, 2)),
-            dma((chunks, 2)),
-            dma((chunks, 2)),
+            dma((spans, 2)),
+            dma((spans, 2)),
+            dma((spans, 2)),
         ]
     )
     return pl.pallas_call(
         kernel,
         out_shape=(
-            jax.ShapeDtypeStruct((tr, tc, bins), bf16),
+            jax.ShapeDtypeStruct((tc, bins, tr), bf16),
             jax.ShapeDtypeStruct((tr, width), bf16),
         ),
-        in_specs=[any_spec()] + [full_spec()] * 10 + [any_spec()] * 9,
+        in_specs=[any_spec()] * 20,
         out_specs=(full_spec(),) * 2,
         scratch_shapes=scratch,
         compiler_params=pltpu.CompilerParams(collective_id=0, has_side_effects=True),
     )(*operands)
+
+
+def hand_over(distogram, seq_out):
+    pieces = 4
+    part = distogram.shape[0] // pieces
+
+    def kernel(big_in, small_in, big_out, small_out, big, small, sem_in, sem_out):
+        def moves(n):
+            at = pl.ds(n * part, part)
+            return (
+                pltpu.make_async_copy(big_in.at[at], big.at[at], sem_in.at[n]),
+                pltpu.make_async_copy(big.at[at], big_out.at[at], sem_out.at[n]),
+            )
+
+        steps = [moves(n) for n in range(pieces)] + [
+            (
+                pltpu.make_async_copy(small_in, small, sem_in.at[pieces]),
+                pltpu.make_async_copy(small, small_out, sem_out.at[pieces]),
+            )
+        ]
+        for take, _ in steps:
+            take.start()
+        for take, give in steps:
+            take.wait()
+            give.start()
+        for _, give in steps:
+            give.wait()
+
+    arrays = (distogram, seq_out)
+    shapes = [jax.ShapeDtypeStruct(x.shape, x.dtype) for x in arrays]
+    return pl.pallas_call(
+        kernel,
+        out_shape=shapes,
+        in_specs=[any_spec()] * 2,
+        out_specs=[any_spec()] * 2,
+        scratch_shapes=[pltpu.VMEM(x.shape, x.dtype) for x in arrays]
+        + [pltpu.SemaphoreType.DMA((pieces + 1,))] * 2,
+    )(*arrays)
 
 
 def per_device(
@@ -648,11 +731,11 @@
     down_weight,
     distance_weight,
 ):
-    return trunk(
+    distogram, seq_out = trunk(
         pair_state,
         seq_state,
-        residue_index.reshape(1, -1),
-        residue_mask.reshape(1, -1),
+        residue_index,
+        residue_mask,
         position_table,
         (attention_gain, bias_norm_gain, outer_gain, transition_gain),
         jnp.swapaxes(bias_weight, 1, 2),
@@ -669,6 +752,8 @@
             down_weight,
         ),
     )
+    distogram, seq_out = hand_over(distogram, seq_out)
+    return distogram.transpose(2, 0, 1), seq_out
 
 
 def solution(mesh):

time: 91.9 us -> 81.6 us (0.89)
  local copies, waits for them, and re-layouts: 5.55 us -> 0 us
  Pallas kernels: 84.1 us -> 79.7 us
    pallas_call x1 -> x2, Pallas kernels: 84.1 us -> 79.7 us  [the longest x1 77.7 us: trunk(): pl.pallas_call(kernel, out_shape=(jax.ShapeDtypeStruct((tc, bins, tr), bf...]
    reshape x2 -> x0, local copies, waits for them, and re-layouts: 2.49 us -> none  [the longest x1 1.25 us: per_device(): residue_index.reshape(1, -1)]
    pallas_call x1 -> x0, local copies, waits for them, and re-layouts: 2.45 us -> none  [trunk(): pl.pallas_call(kernel, out_shape=(jax.ShapeDtypeStruct((tr, tc, bins), bf...]
where the time goes in v2:
time: 81.6 us; the launch traced here: 80.5 us
  Pallas kernels  79.7 us (98%)
    pallas_call x1, Pallas kernels, trunk(): pl.pallas_call(kernel, out_shape=(jax.ShapeDtypeStruct((tc, bins, tr), bf...  77.7 us
    pallas_call x1, Pallas kernels, hand_over(): pl.pallas_call(kernel, out_shape=shapes, in_specs=[any_spec()] * 2, out_s...  1.98 us

profile of v2, /device:TPU:5, one launch (start us, length us, event | category | flops | bytes accessed | tf_op | source)
XLA Modules:
  0.0 80.5 jit_solution(1717068240042606368)
XLA Ops:
  0.6 77.7 %shard_map.203 = (bf16[48,64,96]{2,1,0:T(8,128)(2,1)}, bf16[96,128]{1,0:T(8,128)(2,1)}) custom-call(bf16[96,48,128]{2,1,0:T(8,128)(2,1)} %refs_0_.1, bf16[96,128]{1,0:T(8,128)(2,1)} %refs_1_.1, s32[384]{0:T(512)} %refs_2_.1, s32[384]{0:T(512)} %refs_3_.1, bf16[66,128]{1,0:T(8,128)(2,1)} %refs_4_.1, f32[2,1024]{1,0:T(2,128)} %refs_5_.1, f32[2,128]{1,0:T(2,128)} %refs_6_.1, ...), custom_call_target="tpu_custom_call" | custom-call | tf_op jit(solution)/shard_map/pallas_call | solution.py:661
  78.3 2.0 %shard_map.204 = (bf16[48,64,96]{2,1,0:T(8,128)(2,1)}, bf16[96,128]{1,0:T(8,128)(2,1)}) custom-call(bf16[48,64,96]{2,1,0:T(8,128)(2,1)} %get-tuple-element.6.big_in, bf16[96,128]{1,0:T(8,128)(2,1)} %get-tuple-element.7.small_in), custom_call_target="tpu_custom_call" | custom-call | tf_op jit(solution)/shard_map/pallas_call | solution.py:702

commit v3 on v2

--- a/solution.py
+++ b/solution.py
@@ -9,7 +9,6 @@
 RELPOS_MAX = 32
 MESH = pl.DeviceIdType.MESH
 OWN = 16
-PIECE = 8
 FAR = 1e6
 
 
@@ -47,7 +46,7 @@
     return pl.ds(pl.multiple_of(start, step), size)
 
 
-def trunk(pair_state, seq_tile, index, mask, table, gains, bias_weight_t, dist_t, mats):
+def trunk(pair_state, pair_halves, seq_tile, index, mask, table, gains, bias_weight_t, dist_t, mats):
     nr, nc = lax.axis_size("row"), lax.axis_size("col")
     tr, tc, ch = pair_state.shape
     width = seq_tile.shape[1]
@@ -57,18 +56,18 @@
     length = nr * tr
     lanes = (tr + 127) // 128 * 128
     owners, per, parts = tr // OWN, tc // OWN, tr // tc
-    chunks, spans, half = tc // OWN, tc // PIECE, tc // 2
+    chunks = tc // OWN
     wide = mats[5].shape[2]
     bins = dist_t.shape[0]
-    packed_rows = PIECE * half
-    depth = packed_rows // nc
+    span = OWN * tc
+    sub = span // nc
     score_scale = HEAD_DIM ** (-0.5)
     gap = OWN + 8
     f32, bf16 = jnp.float32, jnp.bfloat16
 
     def kernel(*refs):
         it = iter(refs)
-        pair_hbm, seq_hbm = (next(it) for _ in range(2))
+        pair_hbm, halves_hbm, seq_hbm = (next(it) for _ in range(3))
         small_hbm = [next(it) for _ in range(9)]
         q_hbm, k_hbm, v_hbm, g_hbm, out_hbm = (next(it) for _ in range(5))
         late_hbm = [next(it) for _ in range(4)]
@@ -79,12 +78,12 @@
         q_w, k_w, v_w, g_w = (next(it) for _ in range(4))
         late_refs = [next(it) for _ in range(4)]
         outer_w, mix_w, up_w, down_w = late_refs
-        pair_in, natural, pair_s, mixed, place, table_s, bins_s = (next(it) for _ in range(7))
-        home_w, mirror_s, score_s = (next(it) for _ in range(3))
+        pair_in, natural, pair_s, mixed, place, table_s = (next(it) for _ in range(6))
+        head_w, mirror_s, score_s, own_b, mirror_b = (next(it) for _ in range(5))
         gathered, kv_all, bias_out, bias_all, query_s, gate_s, normed_s = (next(it) for _ in range(7))
         wrow, stage, rs_recv, new_rows, lr_s, left_all, right_all = (next(it) for _ in range(7))
-        left_dup, right_rep, seq_next, out_stage = (next(it) for _ in range(4))
-        flat, spread_s, moved, landed, unpacked = (next(it) for _ in range(5))
+        left_dup, right_rep, left_rep, right_dup, seq_next, out_stage = (next(it) for _ in range(6))
+        spread_s, moved, landed = (next(it) for _ in range(3))
         load_sem, small_sem, seq_sem, w_sem, bias_send, bias_recv, kv_sem = (next(it) for _ in range(7))
         rs_sem, left_sem, right_sem, next_sem, out_sem = (next(it) for _ in range(5))
         one_sem, two_sem, three_sem = (next(it) for _ in range(3))
@@ -150,11 +149,6 @@
             ).start()
         own_seq = pltpu.make_async_copy(seq_hbm, gathered.at[col], seq_sem.at[2])
         own_seq.start()
-        own_w = pltpu.make_async_copy(
-            out_hbm.at[:, rows_at(col * width, width, width), :], wrow.at[col], w_sem.at[2]
-        )
-        own_w.start()
-
         for load in small:
             load.wait()
         coded = jnp.where(mask_ref[...] > 0, index_ref[...].astype(f32), FAR).reshape(1, length)
@@ -164,17 +158,8 @@
         table_s[...] = jnp.zeros_like(table_s)
         table_s[0 : table_ref.shape[0], :] = table_ref[...].astype(f32)
         table_rows = table_s[...].astype(bf16)
-        bins_s[...] = jnp.zeros_like(bins_s)
-        bins_s[0:bins, 0:ch] = dist_ref[...]
-        bins_s[bins : 2 * bins, ch : 2 * ch] = dist_ref[...]
-        home_w[...] = jnp.zeros_like(home_w)
-        unit = lax.broadcasted_iota(jnp.int32, (bins, bins), 0) == lax.broadcasted_iota(
-            jnp.int32, (bins, bins), 1
-        )
-        unit = jnp.where(unit, 1.0, 0.0).astype(bf16)
-        for n in range(2):
-            home_w[n, :, 0:ch] = dist_ref[...]
-            home_w[n, :, ch + n * bins : ch + (n + 1) * bins] = unit
+        head_w[:, 0:ch] = dist_ref[...]
+        head_w[:, ch : 2 * ch] = dist_ref[...]
         lane = lax.broadcasted_iota(jnp.int32, (1, ch), 1).astype(f32)
         shift = lane - (RELPOS_MAX + 1)
         least = jnp.where(lane == 0, -4 * FAR, jnp.where(lane == 1, -FAR / 2, shift))
@@ -228,14 +213,19 @@
                 bias_of(0, normed[j * tr : (j + 1) * tr], j)
             send_bias(0, k)
 
-        def swap_weights():
+        def swap_weights(layer):
+            pltpu.make_async_copy(
+                out_hbm.at[layer, rows_at(col * width, width, width), :],
+                wrow.at[layer, col],
+                w_sem.at[layer, 2],
+            ).start()
             for step in range(1, nc):
                 peer = lax.rem(col + step, nc)
                 remote(
-                    out_hbm.at[:, rows_at(peer * width, width, width), :],
-                    wrow.at[col],
-                    w_sem.at[0],
-                    w_sem.at[1],
+                    out_hbm.at[layer, rows_at(peer * width, width, width), :],
+                    wrow.at[layer, col],
+                    w_sem.at[layer, 0],
+                    w_sem.at[layer, 1],
                     {"col": peer},
                 ).start()
 
@@ -291,10 +281,9 @@
                 )
                 attended = jnp.where(own, mixture, attended)
             gated = (gate_s[...] * attended).astype(bf16)
-            if layer == 0:
-                own_w.wait()
-                settle(wrow.at[pl.ds(0, nc - 1)], w_sem.at[1])
-            weight = jnp.concatenate([wrow[p, layer] for p in range(nc)], axis=1)
+            settle(wrow.at[layer, 0], w_sem.at[layer, 2])
+            settle(wrow.at[layer, pl.ds(0, nc - 1)], w_sem.at[layer, 1])
+            weight = jnp.concatenate([wrow[layer, p] for p in range(nc)], axis=1)
             partial = jnp.dot(gated, weight, preferred_element_type=f32)
             stage[layer] = partial.reshape(owners, OWN, cs).astype(bf16)
             for step in range(owners):
@@ -392,182 +381,207 @@
             def _():
                 right_all[layer] = left_all[layer, rows_at(part_at * tc, tc, OWN), :]
 
-            left = left_all[layer].astype(f32)
-            left_dup[...] = jnp.where(low, left, pltpu.roll(left, ch // 2, axis=1))
-            right = right_all[layer].astype(f32)
-            right = jnp.where(low, pltpu.roll(right, ch // 2, axis=1), right)
+            def both(values):
+                turned = pltpu.roll(values, ch // 2, axis=1)
+                return jnp.where(low, values, turned), jnp.where(low, turned, values)
+
+            left, right = both(left_all[layer].astype(f32))
+            left_dup[...] = left
+            right_dup[layer] = right
+            left, right = both(right_all[layer].astype(f32))
+            left_rep[layer] = jnp.broadcast_to(left[:, None, :], (tc, 8, ch))
             right_rep[...] = jnp.broadcast_to(right[:, None, :], (tc, 8, ch))
 
-        def update(layer, k, count):
-            at = slice(k * count * tr, (k + 1) * count * tr)
-            right = right_rep[k * count : (k + 1) * count][:, None]
-            left = left_dup[...].reshape(1, tr // 8, 8, ch)
+        def features_of(left, right):
             features = jnp.where(low.reshape(1, 1, 1, ch), left * right, left - right)
-            features = features.reshape(count * tr, ch).astype(bf16)
-            middle = pair_s[at, :] + jnp.dot(features, mix_w[layer], preferred_element_type=f32)
+            return features.reshape(-1, ch).astype(bf16)
+
+        def passed(layer, before, features):
+            middle = before + jnp.dot(features, mix_w[layer], preferred_element_type=f32)
             normed = normalize(middle, trans_gain[layer : layer + 1, :]).astype(bf16)
             hidden = jnp.maximum(
                 jnp.dot(normed, up_w[layer], preferred_element_type=f32), 0.0
             ).astype(bf16)
-            fresh = (
-                middle + jnp.dot(hidden, down_w[layer], preferred_element_type=f32)
-            ).astype(bf16)
-            value = fresh.astype(f32)
-            pair_s[at, :] = value
-            if layer < layers - 1:
+            return (middle + jnp.dot(hidden, down_w[layer], preferred_element_type=f32)).astype(
+                bf16
+            )
+
+        def update(layer, first, count):
+            at = slice(first * tr, (first + count) * tr)
+            right = right_rep[first : first + count][:, None]
+            left = left_dup[...].reshape(1, tr // 8, 8, ch)
+            fresh = passed(layer, pair_s[at, :], features_of(left, right))
+            if layer == layers - 1:
+                own_b[at, :] = fresh
+            else:
+                value = fresh.astype(f32)
+                pair_s[at, :] = value
                 normed = normalize(value, bias_gain[layer + 1 : layer + 2, :]).astype(bf16)
                 for n in range(count):
                     bias_of(layer + 1, normed[n * tr : (n + 1) * tr], n)
 
-        def logits(k):
-            for s in range(parts):
-                sides = [
-                    jnp.concatenate(
-                        [
-                            pair_s[pl.ds((k * PIECE + j) * tr + s * tc + n * half, half), :]
-                            for j in range(PIECE)
-                        ],
-                        axis=0,
-                    )
-                    for n in range(2)
-                ]
-                packed = lax.dot_general(
-                    jnp.concatenate(sides, axis=1).astype(bf16),
-                    bins_s[...],
-                    (((1,), (1,)), ((), ())),
-                    preferred_element_type=f32,
-                ).astype(bf16)
-                for p in range(nc):
-                    flat[k, p, s] = packed[p * depth : (p + 1) * depth]
+        def away(g):
+            pltpu.make_async_copy(
+                halves_hbm.at[:, rows_at(g * span + col * sub, sub, 8), :],
+                spread_s.at[g, col],
+                one_sem.at[g, 2],
+            ).start()
             for step in range(1, nc):
                 peer = lax.rem(col + step, nc)
                 remote(
-                    flat.at[k, peer],
-                    spread_s.at[k, col],
-                    one_sem.at[k, 0],
-                    one_sem.at[k, 1],
+                    halves_hbm.at[:, rows_at(g * span + peer * sub, sub, 8), :],
+                    spread_s.at[g, col],
+                    one_sem.at[g, 0],
+                    one_sem.at[g, 1],
                     {"col": peer},
                 ).start()
 
-        def across(k):
-            settle(spread_s.at[k, pl.ds(0, nc - 1)], one_sem.at[k, 1])
+        def across(g):
+            settle(spread_s.at[g, 0], one_sem.at[g, 2])
+            settle(spread_s.at[g, pl.ds(0, nc - 1)], one_sem.at[g, 1])
             for step in range(nc):
                 origin = lax.rem(col + step, nc)
                 peer, slot = lax.div(origin, parts), lax.rem(origin, parts)
-                source = spread_s.at[k, origin] if step else flat.at[k, col]
-                target = moved.at[k, row, slot]
+                source, target = spread_s.at[g, origin], moved.at[g, row, slot]
 
                 @pl.when(peer != row)
                 def _(source=source, target=target, peer=peer):
                     remote(
-                        source, target, two_sem.at[k, 0], two_sem.at[k, 1], {"row": peer}
+                        source, target, two_sem.at[g, 0], two_sem.at[g, 1], {"row": peer}
                     ).start()
 
                 @pl.when(peer == row)
                 def _(source=source, target=target):
-                    pltpu.make_async_copy(source, target, two_sem.at[k, 1]).start()
-
-        def home(k):
-            settle(moved.at[k], two_sem.at[k, 1])
+                    pltpu.make_async_copy(source, target, two_sem.at[g, 1]).start()
+
+        def home(g):
+            settle(moved.at[g], two_sem.at[g, 1])
             for step in range(nr):
                 origin = lax.rem(row + step, nr)
                 for s in range(parts):
                     peer = origin * parts + s
                     for slot in range(parts):
-                        source = moved.at[k, origin, slot, s]
-                        target = landed.at[k, slot, col]
+                        source = moved.at[g, origin, slot, s]
+                        target = landed.at[g, slot, col]
 
                         @pl.when(peer != col)
                         def _(source=source, target=target, peer=peer):
                             remote(
                                 source,
                                 target,
-                                three_sem.at[k, 0],
-                                three_sem.at[k, 1],
+                                three_sem.at[g, 0],
+                                three_sem.at[g, 1],
                                 {"col": peer},
                             ).start()
 
                         @pl.when(peer == col)
                         def _(source=source, target=target):
-                            pltpu.make_async_copy(source, target, three_sem.at[k, 1]).start()
-
-        def collect(k):
-            settle(landed.at[k], three_sem.at[k, 1])
+                            pltpu.make_async_copy(source, target, three_sem.at[g, 1]).start()
+
+        def enter_mirror(g):
+            settle(landed.at[g], three_sem.at[g, 1])
             for slot in range(parts):
-                for p in range(nc):
-                    unpacked[k % 2, slot, p * depth : (p + 1) * depth, :] = landed[
-                        k, slot, p
-                    ].astype(f32)
-
-            @pl.loop(0, half, unroll=8)
-            def _(n):
-                for slot in range(parts):
-                    start = slot * tc + k * PIECE
-                    mirror_s[n, start : start + PIECE, :] = unpacked[
-                        k % 2, slot, pl.ds(n, PIECE, stride=half), :
-                    ]
+                col_pos = place[rows_at(row * tr + slot * tc, tc, 8), :]
+                col_pos = jnp.where(col_pos < FAR, col_pos, -FAR)
+                hots = []
+                for j in range(OWN):
+                    offset = col_pos - place[pl.ds(col * tc + g * OWN + j, 1), :]
+                    hot = (offset >= least) & (offset <= most)
+                    hots.append(jnp.where(hot, 1.0, 0.0))
+                hots = jnp.concatenate(hots, axis=0).astype(bf16)
+                mirror_s[slot, g * span : (g + 1) * span, :] = landed[g, slot].astype(
+                    f32
+                ).reshape(span, ch) + jnp.dot(hots, table_rows, preferred_element_type=f32)
+
+        def update_mirror(layer, g, count):
+            at = slice(g * count * tc, (g + 1) * count * tc)
+            left = left_rep[layer, g * count : (g + 1) * count][:, None]
+            features, before = [], []
+            for slot in range(parts):
+                right = right_dup[layer, slot * tc : (slot + 1) * tc, :]
+                features.append(features_of(left, right.reshape(1, tc // 8, 8, ch)))
+                before.append(mirror_s[slot, at, :])
+            fresh = passed(
+                layer, jnp.concatenate(before, axis=0), jnp.concatenate(features, axis=0)
+            )
+            for slot in range(parts):
+                piece = fresh[slot * count * tc : (slot + 1) * count * tc]
+                if layer == layers - 1:
+                    mirror_b[slot, at, :] = piece
+                else:
+                    mirror_s[slot, at, :] = piece.astype(f32)
 
         def combine():
-            @pl.loop(0, half, unroll=4)
-            def _(n):
-                mirrored = mirror_s[n].astype(bf16)
-                for side in range(2):
-                    j = n + side * half
-                    own = pair_s[rows_at(j * tr, tr, 8), :].astype(bf16)
-                    total = lax.dot_general(
-                        home_w[side],
-                        jnp.concatenate([own, mirrored], axis=1),
-                        (((1,), (1,)), ((), ())),
-                        preferred_element_type=f32,
-                    )
-                    final_ref[j] = (total * 0.5).astype(bf16)
-
+            for j in range(tc):
+                mirrored = jnp.concatenate(
+                    [mirror_b[slot, j * tc : (j + 1) * tc, :] for slot in range(parts)], axis=0
+                )
+                total = lax.dot_general(
+                    head_w[...],
+                    jnp.concatenate([own_b[j * tr : (j + 1) * tr, :], mirrored], axis=1),
+                    (((1,), (1,)), ((), ())),
+                    preferred_element_type=f32,
+                )
+                final_ref[j] = (total * 0.5).astype(bf16)
+
+        swap_weights(0)
         pair_load.wait()
         enter(0)
         own_seq.wait()
         settle(gathered.at[pl.ds(0, nc - 1)], seq_sem.at[1])
         project(0, jnp.concatenate([gathered[p] for p in range(nc)], axis=1).astype(f32))
-        swap_weights()
         for k in range(1, chunks):
             enter(k)
+        away(0)
         project_rest(0)
         for layer in range(layers):
+            last = layer == layers - 1
             attend(layer)
             if layer == 0:
                 for load in loads[4:]:
                     load.wait()
+                away(1)
+            if last:
+                across(2)
+                enter_mirror(0)
+                for below in range(layers - 1):
+                    update_mirror(below, 0, OWN)
             finish_rows(layer)
+            if layer == 0:
+                across(0)
+                swap_weights(1)
+            if last:
+                home(1)
             sides(layer)
-            if layer < layers - 1:
+            if not last:
+                away(2)
                 for k in range(chunks):
-                    update(layer, k, OWN)
+                    update(layer, k * OWN, OWN)
                     send_bias(layer + 1, k)
                     if k == 0:
                         from_owners(seq_next, seq_next.at[some], next_sem.at[1])
                         project(layer + 1, seq_next[...].astype(f32))
+                        across(1)
+                home(0)
                 project_rest(layer + 1)
-        for k in range(spans):
-            update(layers - 1, k, PIECE)
-            logits(k)
-            if k >= 1:
-                across(k - 1)
-            if k >= 3:
-                home(k - 3)
-            if k >= 5:
-                collect(k - 5)
-        across(spans - 1)
-        for k in range(max(spans - 3, 0), spans):
-            home(k)
-            if k >= 2:
-                collect(k - 2)
-        for k in range(max(spans - 2, 0), spans):
-            collect(k)
+        update(layers - 1, 0, OWN)
+        home(2)
+        update(layers - 1, OWN, tc - OWN)
+        update_mirror(layers - 1, 0, OWN)
+        enter_mirror(1)
+        for below in range(layers - 1):
+            update_mirror(below, 1, OWN)
+        update_mirror(layers - 1, 1, OWN)
+        enter_mirror(2)
+        for below in range(layers - 1):
+            update_mirror(below, 2, OWN)
+        update_mirror(layers - 1, 2, OWN)
         combine()
         from_owners(seq_out, seq_out.at[some], out_sem.at[1])
 
         settle(gathered.at[pl.ds(0, nc - 1)], seq_sem.at[0])
-        settle(wrow.at[pl.ds(0, nc - 1)], w_sem.at[0])
         for layer in range(layers):
+            settle(wrow.at[layer, pl.ds(0, nc - 1)], w_sem.at[layer, 0])
             for k in range(chunks):
                 settle(
                     bias_out.at[layer, pl.ds(0, (nc - 1) * hl), pl.ds(k * OWN, OWN)],
@@ -594,17 +608,17 @@
                 else:
                     settle(out_stage.at[pl.ds(0, nc - 1)], out_sem.at[0])
 
-        for k in range(spans):
-            settle(flat.at[k, pl.ds(0, nc - 1)], one_sem.at[k, 0])
-            settle(flat.at[k, pl.ds(0, nc - parts)], two_sem.at[k, 0])
-            settle(landed.at[k, :, pl.ds(0, nc - 1)], three_sem.at[k, 0])
+        for g in range(chunks):
+            settle(spread_s.at[g, pl.ds(0, nc - 1)], one_sem.at[g, 0])
+            settle(spread_s.at[g, pl.ds(0, nc - parts)], two_sem.at[g, 0])
+            settle(landed.at[g, :, pl.ds(0, nc - 1)], three_sem.at[g, 0])
 
     operands = (
-        pair_state, seq_tile, index, mask, table, *gains, bias_weight_t, dist_t, *mats,
+        pair_state, pair_halves, seq_tile, index, mask, table, *gains, bias_weight_t, dist_t, *mats,
     )
     vm, dma = pltpu.VMEM, pltpu.SemaphoreType.DMA
     scratch = (
-        [vm(x.shape, x.dtype) for x in operands[2:11]]
+        [vm(x.shape, x.dtype) for x in operands[3:12]]
         + [vm((layers, cs, width), bf16)] * 4
         + [vm(m.shape, bf16) for m in mats[5:]]
         + [
@@ -614,10 +628,11 @@
             vm((OWN * heads, lanes), f32),
             vm((length, 128), f32),
             vm(((table.shape[0] + 127) // 128 * 128, ch), f32),
-            vm((2 * bins, 2 * ch), bf16),
-            vm((2, bins, 2 * ch), bf16),
-            vm((half, tr, 2 * bins), f32),
+            vm((bins, 2 * ch), bf16),
+            vm((parts, tc * tc, ch), f32),
             vm((hl, length, lanes), f32),
+            vm((tc * tr, ch), bf16),
+            vm((parts, tc * tc, ch), bf16),
             vm((nc, tr, width), bf16),
             vm((layers, nr, 2, tr, width), bf16),
             vm((layers, heads, tc, lanes), bf16),
@@ -625,7 +640,7 @@
             vm((tr, width), bf16),
             vm((tr, width), f32),
             vm((tr, cs), bf16),
-            vm((nc, layers, width, width), bf16),
+            vm((layers, nc, width, width), bf16),
             vm((layers, owners, OWN, cs), bf16),
             vm((layers, nc, OWN, cs), bf16),
             vm((layers, OWN, cs), bf16),
@@ -634,17 +649,17 @@
             vm((layers, tc, wide), bf16),
             vm((tr, ch), f32),
             vm((tc, 8, ch), f32),
+            vm((layers, tc, 8, ch), f32),
+            vm((layers, tr, ch), f32),
             vm((tr, cs), bf16),
             vm((nc, OWN, width), bf16),
-            vm((spans, nc, parts, depth, 2 * bins), bf16),
-            vm((spans, nc, parts, depth, 2 * bins), bf16),
-            vm((spans, nr, parts, parts, depth, 2 * bins), bf16),
-            vm((spans, parts, nc, depth, 2 * bins), bf16),
-            vm((2, parts, packed_rows, 2 * bins), f32),
+            vm((chunks, nc, parts, sub, ch), bf16),
+            vm((chunks, nr, parts, parts, sub, ch), bf16),
+            vm((chunks, parts, nc, sub, ch), bf16),
             dma((9,)),
             dma((9,)),
             dma((3,)),
-            dma((3,)),
+            dma((layers, 3)),
             dma((layers, chunks)),
             dma((layers, chunks)),
             dma((layers, 2)),
@@ -653,9 +668,9 @@
             dma((layers, 2)),
             dma((2,)),
             dma((2,)),
-            dma((spans, 2)),
-            dma((spans, 2)),
-            dma((spans, 2)),
+            dma((chunks, 3)),
+            dma((chunks, 2)),
+            dma((chunks, 2)),
         ]
     )
     return pl.pallas_call(
@@ -664,7 +679,7 @@
             jax.ShapeDtypeStruct((tc, bins, tr), bf16),
             jax.ShapeDtypeStruct((tr, width), bf16),
         ),
-        in_specs=[any_spec()] * 20,
+        in_specs=[any_spec()] * len(operands),
         out_specs=(full_spec(),) * 2,
         scratch_shapes=scratch,
         compiler_params=pltpu.CompilerParams(collective_id=0, has_side_effects=True),
@@ -731,8 +746,10 @@
     down_weight,
     distance_weight,
 ):
+    parts = pair_state.shape[0] // pair_state.shape[1]
     distogram, seq_out = trunk(
         pair_state,
+        pair_state.reshape(parts, -1, pair_state.shape[2]),
         seq_state,
         residue_index,
         residue_mask,

time: 81.6 us -> 75.6 us (0.926); the launches traced: 80.5 us -> 75.4 us
  Pallas kernels: 79.7 us -> 74.6 us
    pallas_call x1, Pallas kernels: 77.7 us -> 72.6 us  [trunk(): pl.pallas_call(kernel, out_shape=(jax.ShapeDtypeStruct((tc, bins, tr), bf...]
where the time goes in v3:
time: 75.6 us; the launch traced here: 75.4 us
  Pallas kernels  74.6 us (99%)
  between operations  0.81 us (1%)
    pallas_call x1, Pallas kernels, trunk(): pl.pallas_call(kernel, out_shape=(jax.ShapeDtypeStruct((tc, bins, tr), bf...  72.6 us
    pallas_call x1, Pallas kernels, hand_over(): pl.pallas_call(kernel, out_shape=shapes, in_specs=[any_spec()] * 2, out_s...  1.98 us

profile of v3, /device:TPU:5, one launch (start us, length us, event | category | flops | bytes accessed | tf_op | source)
XLA Modules:
  0.0 75.4 jit_solution(13160136390618334036)
XLA Ops:
  0.6 72.6 %shard_map.203 = (bf16[48,64,96]{2,1,0:T(8,128)(2,1)}, bf16[96,128]{1,0:T(8,128)(2,1)}) custom-call(bf16[96,48,128]{2,1,0:T(8,128)(2,1)} %refs_0_.1, bf16[2,2304,128]{2,1,0:T(8,128)(2,1)} %bitcast.4, bf16[96,128]{1,0:T(8,128)(2,1)} %refs_2_.1, s32[384]{0:T(512)} %refs_3_.1, s32[384]{0:T(512)} %refs_4_.1, bf16[66,128]{1,0:T(8,128)(2,1)} %refs_5_.1, ...), custom_call_target="tpu_custom_call" | custom-call | tf_op jit(solution)/shard_map/pallas_call | solution.py:676
  73.3 2.0 %shard_map.204 = (bf16[48,64,96]{2,1,0:T(8,128)(2,1)}, bf16[96,128]{1,0:T(8,128)(2,1)}) custom-call(bf16[48,64,96]{2,1,0:T(8,128)(2,1)} %get-tuple-element.6.big_in, bf16[96,128]{1,0:T(8,128)(2,1)} %get-tuple-element.7.small_in), custom_call_target="tpu_custom_call" | custom-call | tf_op jit(solution)/shard_map/pallas_call | solution.py:717

commit v4 on v3

--- a/solution.py
+++ b/solution.py
@@ -549,11 +549,11 @@
             finish_rows(layer)
             if layer == 0:
                 across(0)
-                swap_weights(1)
             if last:
                 home(1)
             sides(layer)
             if not last:
+                swap_weights(1)
                 away(2)
                 for k in range(chunks):
                     update(layer, k * OWN, OWN)
@@ -567,11 +567,10 @@
         update(layers - 1, 0, OWN)
         home(2)
         update(layers - 1, OWN, tc - OWN)
-        update_mirror(layers - 1, 0, OWN)
         enter_mirror(1)
         for below in range(layers - 1):
             update_mirror(below, 1, OWN)
-        update_mirror(layers - 1, 1, OWN)
+        update_mirror(layers - 1, 0, 2 * OWN)
         enter_mirror(2)
         for below in range(layers - 1):
             update_mirror(below, 2, OWN)

time: 75.6 us -> 75.4 us (level)
  no operation moved by 1% of the time
where the time goes in v4:
time: 75.4 us; the launch traced here: 75.3 us
  Pallas kernels  74.5 us (99%)
  between operations  0.81 us (1%)
    pallas_call x1, Pallas kernels, trunk(): pl.pallas_call(kernel, out_shape=(jax.ShapeDtypeStruct((tc, bins, tr), bf...  72.5 us
    pallas_call x1, Pallas kernels, hand_over(): pl.pallas_call(kernel, out_shape=shapes, in_specs=[any_spec()] * 2, out_s...  1.98 us

profile of v4, /device:TPU:5, one launch (start us, length us, event | category | flops | bytes accessed | tf_op | source)
XLA Modules:
  0.0 75.3 jit_solution(13316179700718937185)
XLA Ops:
  0.6 72.5 %shard_map.203 = (bf16[48,64,96]{2,1,0:T(8,128)(2,1)}, bf16[96,128]{1,0:T(8,128)(2,1)}) custom-call(bf16[96,48,128]{2,1,0:T(8,128)(2,1)} %refs_0_.1, bf16[2,2304,128]{2,1,0:T(8,128)(2,1)} %bitcast.4, bf16[96,128]{1,0:T(8,128)(2,1)} %refs_2_.1, s32[384]{0:T(512)} %refs_3_.1, s32[384]{0:T(512)} %refs_4_.1, bf16[66,128]{1,0:T(8,128)(2,1)} %refs_5_.1, ...), custom_call_target="tpu_custom_call" | custom-call | tf_op jit(solution)/shard_map/pallas_call | solution.py:675
  73.1 2.0 %shard_map.204 = (bf16[48,64,96]{2,1,0:T(8,128)(2,1)}, bf16[96,128]{1,0:T(8,128)(2,1)}) custom-call(bf16[48,64,96]{2,1,0:T(8,128)(2,1)} %get-tuple-element.6.big_in, bf16[96,128]{1,0:T(8,128)(2,1)} %get-tuple-element.7.small_in), custom_call_target="tpu_custom_call" | custom-call | tf_op jit(solution)/shard_map/pallas_call | solution.py:716
